TPU v7x, 32 devices: a whole 2x2x4 slice. The times are simulated.
32 devices in a mesh: groups: 2 (over x), ctx: 16 (over z, y, core).
Axes of the slice: x: 2, y: 2, z: 4, core: 2. Of those that a mesh axis runs over, the one named last changes fastest.
Arguments:
- projected: bfloat16 [3, 16384, 4096], P(None, ('groups', 'ctx')), parts along dimension 1, may hold values from -6 to 6
- conv_weight: float32 [3, 4, 4096], replicated, may hold values from -3 to 3
- level_codes: int32 [14, 32, 16384], P(None, None, ('groups', 'ctx')), parts along dimension 2, may hold values from 1 to 16
- out_gain: float32 [4096], replicated, may hold values from 0.25 to 1.75
Outputs:
- mixed: bfloat16 [16384, 4096], P(('groups', 'ctx')), parts along dimension 0
There are 2 independent parts, one for each index of `groups`. A program takes and returns all parts, laid end to end along the dimension named above; an argument that names none is the same for every part. Nothing has to cross between parts.
Inputs may be any that keep to these rules, and one draw needn't show every extreme that they name: `level_codes`: numerators of the level coefficients, which are the values divided by 8.
All inputs are finite; a program needn't handle non-finite values.
Results may differ from a plain program's by a relative error of at most 0.007.
Values may be sent and summed in bfloat16 or wider, within the bound.
A program may use at most 192 MiB of HBM per device.

v0:
```python
import functools

import jax
import jax.numpy as jnp
from jax import lax
from jax.experimental import pallas as pl
from jax.experimental.pallas import tpu as pltpu
from jax.sharding import PartitionSpec as P

PAD = 8
TILE = 128
NT = (((1,), (1,)), ((), ()))


def convolve(data_ref, rim_ref, taps_ref, scratch):
    held, older = scratch.at[0], scratch.at[1]
    rows = data_ref.shape[1]
    taps = taps_ref.shape[1]
    held[PAD - taps + 1 : PAD, :] = rim_ref[0].astype(jnp.float32)
    held[PAD : PAD + rows, :] = data_ref[0].astype(jnp.float32)
    weight = [taps_ref[0, tap : tap + 1, :] for tap in range(taps)]
    last = slice(PAD, PAD + rows)
    before = held[PAD - 1 : PAD - 1 + rows, :]
    if taps == 4:
        older[PAD - 2 : PAD, :] = (
            weight[1] * held[PAD - 2 : PAD, :] + weight[0] * held[PAD - 3 : PAD - 1, :]
        )
        older[last, :] = weight[1] * held[last, :] + weight[0] * before
        total = older[PAD - 2 : PAD - 2 + rows, :]
        total = total + weight[2] * before + weight[3] * held[last, :]
    else:
        total = weight[0] * held[PAD - taps + 1 : PAD - taps + 1 + rows, :]
        for tap in range(1, taps):
            first = PAD - taps + 1 + tap
            total = total + weight[tap] * held[first : first + rows, :]
    return total.astype(jnp.bfloat16)


def state_kernel(dim, k_in, v_in, k_rim, v_rim, k_taps, v_taps, k_out, vt_out, state_out, held):
    k_out[...] = convolve(k_in, k_rim, k_taps, held)
    values = convolve(v_in, v_rim, v_taps, held)
    for head in range(k_out.shape[1] // dim):
        lanes = slice(head * dim, (head + 1) * dim)
        flipped = values[:, lanes].T
        vt_out[lanes, :] = flipped
        state_out[head] = jnp.dot(
            flipped, k_out[:, lanes], preferred_element_type=jnp.float32
        ).astype(jnp.bfloat16)


def tile_weights(lam, rows):
    strip = PAD.bit_length() - 1
    query = lax.rem(lax.broadcasted_iota(jnp.int32, (TILE // PAD, rows), 1), TILE)
    block = lax.broadcasted_iota(jnp.int32, (TILE // PAD, rows), 0)
    differ = lax.bitwise_xor(lax.shift_right_logical(query, strip), block)
    top = TILE.bit_length() - 1
    outer = jnp.broadcast_to(lam[top : top + 1], differ.shape)
    for level in range(top - 1, strip, -1):
        outer = jnp.where(differ < 2 ** (level - strip), lam[level : level + 1], outer)
    outer = jnp.where(block <= lax.shift_right_logical(query, strip), outer, 0.0)
    query8 = lax.rem(lax.broadcasted_iota(jnp.int32, (PAD, rows), 1), PAD)
    key8 = lax.broadcasted_iota(jnp.int32, (PAD, rows), 0)
    differ8 = lax.bitwise_xor(query8, key8)
    inner = jnp.broadcast_to(lam[strip : strip + 1], differ8.shape)
    for level in range(strip - 1, -1, -1):
        inner = jnp.where(differ8 < 2**level, lam[level : level + 1], inner)
    inner = jnp.where(key8 <= query8, inner, 0.0)
    own = lax.shift_right_logical(
        lax.rem(lax.broadcasted_iota(jnp.int32, (PAD, rows), 1), TILE), strip
    )
    return jnp.concatenate(
        [
            jnp.where(own == number, inner, outer[number : number + 1])
            for number in range(TILE // PAD)
        ],
        0,
    )


def inside_kernel(dim, q_in, q_rim, q_taps, k_in, vt_in, lam_in, q_old, in_old, q_out, in_out, held, weights):
    rows = k_in.shape[0]
    tiles = rows // TILE
    q_out[...] = convolve(q_in, q_rim, q_taps, held)
    top = TILE.bit_length() - 1
    pair = min(2, tiles)
    for tile in range(tiles):
        start = tile // pair * pair * TILE
        if start < tile * TILE:
            weights[tile * TILE : (tile + 1) * TILE, start : tile * TILE] = jnp.zeros(
                (TILE, tile * TILE - start), jnp.bfloat16
            )
    for head in range(k_in.shape[1] // dim):
        lanes = slice(head * dim, (head + 1) * dim)
        lam = lam_in[head]
        diagonal = tile_weights(lam, rows)
        for tile in range(tiles):
            keys = slice(tile * TILE, (tile + 1) * TILE)
            scores = lax.dot_general(
                k_in[keys, lanes],
                q_out[tile * TILE :, lanes],
                NT,
                preferred_element_type=jnp.float32,
            )
            for other in range(tile, tiles):
                queries = slice(other * TILE, (other + 1) * TILE)
                part = scores[:, (other - tile) * TILE : (other - tile + 1) * TILE]
                if other == tile:
                    factor = diagonal[:, queries]
                else:
                    level = top + (other ^ tile).bit_length()
                    factor = lam[level : level + 1, queries]
                weights[keys, queries] = (part * factor).astype(jnp.bfloat16)
        for first in range(0, tiles, pair):
            queries = slice(first * TILE, (first + pair) * TILE)
            depth = (first + pair) * TILE
            in_out[lanes, queries] = jnp.dot(
                vt_in[lanes, :depth], weights[:depth, queries], preferred_element_type=jnp.float32
            )


def mix_kernel(dim, base, depths, q_in, in_in, lam_in, gain_in, pieces, out):
    place = pl.program_id(0)
    for head in range(q_in.shape[1] // dim):
        lanes = slice(head * dim, (head + 1) * dim)
        chosen = []
        for shift, refs in zip(depths, pieces):
            value = refs[0][head]
            for index in range(1, len(refs)):
                value = jnp.where((place >> shift) == index, refs[index][head], value)
            chosen.append(value)
        total = in_in[lanes, :]
        products = lax.dot_general(
            jnp.concatenate(chosen, 0), q_in[:, lanes], NT, preferred_element_type=jnp.float32
        )
        for bit in range(len(chosen)):
            product = products[bit * dim : (bit + 1) * dim]
            total = total + lam_in[head, base + bit : base + bit + 1, :] * product
        inverse = lax.rsqrt(jnp.mean(total * total, 0, keepdims=True) + 1e-06)
        normed = (total * inverse).T * gain_in[0:1, lanes]
        out[:, lanes] = normed.astype(jnp.bfloat16)


class Chain:
    def __init__(self, deepest):
        self.count = lax.axis_size("ctx")
        self.bits = self.count.bit_length() - 1
        self.me = lax.axis_index("ctx")
        self.deepest = deepest
        self.state, self.cut, self.got = None, 0, {}

    def depth(self, bit):
        return min((bit + 1) // 2, self.deepest, 1)

    def operations(self, bit):
        return [(bit, offset) for offset in range(2 ** self.depth(bit))]

    def takers(self, bit):
        return [to for to in range(self.count) if bit < self.bits - 1 or to >> bit & 1]

    def outgoing(self, operation):
        bit, offset = operation
        if offset:
            return self.got[bit][0]
        while self.cut < self.depth(bit):
            size = self.state.shape[0] // 2
            start = ((self.me >> self.cut) & 1) * size
            self.state = lax.dynamic_slice_in_dim(self.state, start, size, 0)
            self.cut += 1
        return self.state

    def exchange(self, operation, value):
        bit, offset = operation
        depth = self.depth(bit)
        away = sum(2 ** (depth - 1 - step) for step in range(depth) if offset >> step & 1)
        if not offset:
            away = 2**bit
        return lax.ppermute(value, "ctx", [(to ^ away, to) for to in self.takers(bit)])

    def land(self, operation, value, came):
        bit, offset = operation
        if offset:
            self.got[bit].append(came)
            return
        self.got[bit] = [came]
        if bit < self.bits - 1:
            total = value.astype(jnp.float32) + came.astype(jnp.float32)
            self.state = total.astype(jnp.bfloat16)

    def levels(self):
        return [self.got[bit] for bit in range(self.bits)]


def tie(values):
    return lax.optimization_barrier(values)


def stage(moves, compute, inputs):
    values, inputs = tie(([chain.outgoing(op) for chain, op in moves], inputs))
    came = [chain.exchange(op, value) for (chain, op), value in zip(moves, values)]
    results = compute(inputs) if compute else inputs
    came, values, results = tie((came, values, results))
    for (chain, op), value, new in zip(moves, values, came):
        chain.land(op, value, new)
    return results


def spread(groups, rounds):
    half = len(groups) // 2
    early = rounds // 2
    calls = []
    for base, count in ((0, early), (half, rounds - early)):
        for index in range(count):
            start = -(-half * index // count)
            stop = -(-half * (index + 1) // count)
            calls.append([(base + start, stop - start)] if stop > start else [])
    return calls


def on_device(projected, conv_weight, level_codes, out_gain):
    taps = conv_weight.shape[1]
    rows, width = projected.shape[1:]
    level_count, heads = level_codes.shape[:2]
    dim = width // heads
    tok_bits = rows.bit_length() - 1
    count = lax.axis_size("ctx")
    bits = count.bit_length() - 1
    me = lax.axis_index("ctx")
    group = 4
    lanes = group * dim
    halves = 2
    steps = heads // group // halves
    deepest = steps.bit_length() - 1
    own_bits = sum(((me >> step) & 1) << (deepest - 1 - step) for step in range(deepest))
    order = lax.iota(jnp.int32, steps) ^ own_bits

    rim = lax.ppermute(
        projected[:, rows - taps + 1 :, :], "ctx", [(c, c + 1) for c in range(count - 1)]
    )
    on_bit = (me >> jnp.arange(bits)) & 1
    scale = jnp.concatenate([jnp.ones((tok_bits + 1,), jnp.int32), on_bit])
    lam = (level_codes * scale[:, None, None]).transpose(1, 0, 2).astype(jnp.float32) / 8.0
    rim, lam = tie((rim, lam))

    def data(kind, base):
        return [
            pl.BlockSpec((1, rows, lanes), lambda g: (kind, 0, g + base)),
            pl.BlockSpec((1, taps - 1, lanes), lambda g: (kind, 0, g + base)),
            pl.BlockSpec((1, taps, lanes), lambda g: (kind, 0, g + base)),
        ]

    def wide(base=0):
        return pl.BlockSpec((rows, lanes), lambda g: (0, g + base))

    def tall(base=0):
        return pl.BlockSpec((lanes, rows), lambda g: (g + base, 0))

    def per_head(size, base=0):
        return pl.BlockSpec((group,) + size, lambda g: (g + base, 0, 0))

    held = pltpu.VMEM((2, PAD + rows, lanes), jnp.float32)
    limit = pltpu.CompilerParams(vmem_limit_bytes=56 * 2**20)
    half_width = width // halves

    def states(half, rim):
        base = half * steps
        return pl.pallas_call(
            functools.partial(state_kernel, dim),
            grid=(steps,),
            in_specs=[s for both in zip(data(1, base), data(2, base)) for s in both],
            out_specs=[wide(), tall(), per_head((dim, dim))],
            out_shape=[
                jax.ShapeDtypeStruct((rows, half_width), jnp.bfloat16),
                jax.ShapeDtypeStruct((half_width, rows), jnp.bfloat16),
                jax.ShapeDtypeStruct((heads // halves, dim, dim), jnp.bfloat16),
            ],
            scratch_shapes=[held],
            compiler_params=limit,
            cost_estimate=pl.CostEstimate(
                flops=2 * rows * half_width * dim,
                bytes_accessed=8 * rows * half_width,
                transcendentals=0,
            ),
            name="states",
        )(projected, projected, rim, rim, conv_weight, conv_weight)

    def inside(first_group, own, rim, keys, values_t, lam, done):
        within = first_group % steps
        share = rows * rows * lanes * own
        call = pl.pallas_call(
            functools.partial(inside_kernel, dim)
            if done
            else lambda *refs: inside_kernel(dim, *refs[:6], None, None, *refs[6:]),
            grid=(own,),
            in_specs=data(0, first_group)
            + [wide(within), tall(within), per_head((level_count, rows), first_group)]
            + [pl.BlockSpec(memory_space=pl.ANY)] * len(done),
            out_specs=[wide(within), tall(within)],
            out_shape=[
                jax.ShapeDtypeStruct((rows, half_width), jnp.bfloat16),
                jax.ShapeDtypeStruct((half_width, rows), jnp.float32),
            ],
            scratch_shapes=[held, pltpu.VMEM((rows, rows), jnp.bfloat16)],
            input_output_aliases={6: 0, 7: 1} if done else {},
            compiler_params=limit,
            cost_estimate=pl.CostEstimate(
                flops=8 * share, bytes_accessed=10 * rows * lanes * own, transcendentals=0
            ),
            name="inside",
        )
        return list(call(projected, rim, conv_weight, keys, values_t, lam, *done))

    def mix(half, queries, within, lam, levels, done):
        base = half * steps
        shifts = [deepest - len(pieces).bit_length() + 1 for pieces in levels]
        flat = [piece for pieces in levels for piece in pieces]

        def kernel(order, q_in, in_in, lam_in, gain_in, *rest):
            rest = list(rest)
            refs = [[rest.pop(0) for _ in pieces] for pieces in levels]
            mix_kernel(
                dim, tok_bits + 1, shifts, q_in, in_in, lam_in, gain_in, refs, rest[-1]
            )

        def piece_spec(shift):
            return pl.BlockSpec(
                (group, dim, dim), lambda g, order: (order[g] & (2**shift - 1), 0, 0)
            )

        return pl.pallas_call(
            kernel,
            grid_spec=pltpu.PrefetchScalarGridSpec(
                num_scalar_prefetch=1,
                grid=(steps,),
                in_specs=[
                    pl.BlockSpec((rows, lanes), lambda g, order: (0, order[g])),
                    pl.BlockSpec((lanes, rows), lambda g, order: (order[g], 0)),
                    pl.BlockSpec(
                        (group, level_count, rows), lambda g, order: (order[g] + base, 0, 0)
                    ),
                    pl.BlockSpec((1, lanes), lambda g, order: (0, order[g] + base)),
                ]
                + [piece_spec(shift) for shift, pieces in zip(shifts, levels) for _ in pieces]
                + [pl.BlockSpec(memory_space=pl.ANY)] * len(done),
                out_specs=pl.BlockSpec((rows, lanes), lambda g, order: (0, order[g] + base)),
            ),
            out_shape=jax.ShapeDtypeStruct((rows, width), jnp.bfloat16),
            input_output_aliases={5 + len(flat): 0} if done else {},
            compiler_params=limit,
            cost_estimate=pl.CostEstimate(
                flops=2 * bits * rows * half_width * dim,
                bytes_accessed=8 * rows * half_width,
                transcendentals=0,
            ),
            name="mix",
        )(order, queries, within, lam, out_gain.reshape(1, width), *flat, *done)

    first, second = Chain(deepest), Chain(deepest)
    keys, values_t = [None] * halves, [None] * halves
    keys[0], values_t[0], first.state = states(0, rim)
    keys[1], values_t[1], second.state = stage(
        [(first, op) for op in first.operations(0)], lambda r: states(1, r), rim
    )
    plan = {}
    for chain, lag in ((first, 0), (second, 1)):
        for bit in range(bits):
            for op in chain.operations(bit):
                plan.setdefault(bit + lag + (op[1] > 0), []).append((chain, op))
    rounds = max(plan)
    ready = max(turn for turn in plan for chain, _ in plan[turn] if chain is first)
    left = list(range(steps * halves))
    sizes = spread(left, ready)
    done = [[], []]
    for turn in range(1, rounds + 1):
        moves = plan[turn]
        if turn <= ready:
            todo = sizes[turn - 1]

            def run(inputs):
                lam, done = inputs
                done = list(done)
                for start, own in todo:
                    half = start // steps
                    done[half] = inside(
                        start, own, rim, keys[half], values_t[half], lam, done[half]
                    )
                return lam, done

            lam, done = stage(moves, run, (lam, done))
        elif turn == ready + 1:

            def run(inputs):
                lam, (queries, within), levels = inputs
                return mix(0, queries, within, lam, levels, [])

            out = stage(moves, run, (lam, done[0], first.levels()))
        else:
            out = stage(moves, None, out)
    return mix(1, *done[1], lam, second.levels(), [out])


def solution(mesh):
    placed = (P(None, ("groups", "ctx"), None), P(), P(None, None, ("groups", "ctx")), P())
    return jax.shard_map(
        on_device, mesh=mesh, in_specs=placed, out_specs=P(("groups", "ctx"), None), check_vma=False
    )
```

profile of v0, /device:TPU:25, one launch (start us, length us, event | category | flops | bytes accessed | tf_op | source)
XLA Modules:
  0.0 95.6 jit_solution(3538409984759971767)
XLA Ops:
  0.0 1.0 %slice.3 = bf16[3,3,4096]{2,1,0:T(4,128)(2,1)S(1)} slice(bf16[3,512,4096]{2,1,0:T(8,128)(2,1)} %q_in.3), slice={[0:3], [509:512], [0:4096]} | slice | bytes 147456 | tf_op jit(solution)/shard_map/slice | solution.py:237
  1.0 3.7 %collective-permute-start = (bf16[3,3,4096]{2,1,0:T(4,128)(2,1)S(1)}, bf16[3,3,4096]{2,1,0:T(4,128)(2,1)S(1)}, u32[]{:S(2)}, u32[]{:S(2)}) collective-permute-start(bf16[3,3,4096]{2,1,0:T(4,128)(2,1)S(1)} %slice.3), channel_id=1, source_target_pairs={{0,1},{1,2},{2,3},{3,4},{4,5},{5,6},{6,7},{7,8},{8,9},{9,10},{10,1... | collective-permute-start | bytes 221192 | tf_op jit(solution)/shard_map/ppermute | solution.py:236
  4.7 0.1 concatenate.3
  4.8 2.8 %fusion.2.refs_5_.lam_in = f32[32,14,512]{2,1,0:T(8,128)} fusion(s32[14,32,512]{2,1,0:T(8,128)} %param.6, s32[14]{0:T(128)S(1)} %concatenate.3), kind=kLoop, calls=%fused_computation.3 | loop fusion | flops 688128 | bytes 1835064 | tf_op jit(solution)/shard_map/div | solution.py:241
  7.6 0.0 collective-permute-done.k_rim.v_rim.refs_1_.q_rim
  7.6 0.6 copy-done
  8.2 8.3 %states.2 = (bf16[512,2048]{1,0:T(8,128)(2,1)}, bf16[2048,512]{1,0:T(8,128)(2,1)}, bf16[16,128,128]{2,1,0:T(8,128)(2,1)}) custom-call(bf16[3,512,4096]{2,1,0:T(8,128)(2,1)} %q_in.3, bf16[3,512,4096]{2,1,0:T(8,128)(2,1)} %q_in.3, bf16[3,3,4096]{2,1,0:T(4,128)(2,1)} %copy-done, bf16[3,3,4096]{2,1,0:T(4,128)(2,1)} %copy-done, f32[3,4,4096]{2,1,0:T(4,128)} %q_taps.3, ...), custom_call_target="tpu_custom_call" | custom-call | flops 268435456 | bytes 8388608 | tf_op jit(solution)/shard_map/states/pallas_call | solution.py:266
  16.5 0.9 collective-permute-start.1
  17.4 8.2 %states.3 = (bf16[512,2048]{1,0:T(8,128)(2,1)}, bf16[2048,512]{1,0:T(8,128)(2,1)}, bf16[16,128,128]{2,1,0:T(8,128)(2,1)}) custom-call(bf16[3,512,4096]{2,1,0:T(8,128)(2,1)} %q_in.3, bf16[3,512,4096]{2,1,0:T(8,128)(2,1)} %q_in.3, bf16[3,3,4096]{2,1,0:T(4,128)(2,1)} %copy-done, bf16[3,3,4096]{2,1,0:T(4,128)(2,1)} %copy-done, f32[3,4,4096]{2,1,0:T(4,128)} %q_taps.3, ...), custom_call_target="tpu_custom_call" | custom-call | flops 268435456 | bytes 8388608 | tf_op jit(solution)/shard_map/states/pallas_call | solution.py:266
  25.6 0.0 collective-permute-done.1.rest_0_
  25.6 0.0 copy-start.2
  25.6 0.0 copy-done.16
  25.6 0.1 add_convert_fusion.5
  25.7 0.1 collective-permute-start.3
  25.8 0.4 collective-permute-start.2
  26.2 6.3 %inside.4 = (bf16[512,2048]{1,0:T(8,128)(2,1)}, f32[2048,512]{1,0:T(8,128)}) custom-call(bf16[3,512,4096]{2,1,0:T(8,128)(2,1)} %q_in.3, bf16[3,3,4096]{2,1,0:T(4,128)(2,1)} %copy-done, f32[3,4,4096]{2,1,0:T(4,128)} %q_taps.3, bf16[512,2048]{1,0:T(8,128)(2,1)} %get-tuple-element.112.refs_3_.k_in, bf16[2048,512]{1,0:T(8,128)(2,1)} %get-tuple-element.113.refs_4_.vt_in, ...), custom_call_target="tpu_custom_call" | custom-call | flops 2147483648 | bytes 5242880 | tf_op jit(solution)/shard_map/inside/pallas_call | solution.py:310
  32.6 0.0 copy-done.2
  32.6 0.7 collective-permute-done.2.rest_1_
  33.3 0.0 collective-permute-done.3.rest_0_
  33.3 0.0 copy-done.15
  33.3 0.1 add_convert_fusion.3
  33.5 1.4 %collective-permute-start.4 = (bf16[8,128,128]{2,1,0:T(8,128)(2,1)S(1)}, bf16[8,128,128]{2,1,0:T(8,128)(2,1)S(1)}, u32[]{:S(2)}, u32[]{:S(2)}) collective-permute-start(bf16[8,128,128]{2,1,0:T(8,128)(2,1)S(1)} %collective-permute-done.2.rest_1_), channel_id=1, source_target_pairs={{1,0},{0,1},{3,2},{2,3},{5,4},{4,5},{7,6},{6,7},{9,8},{8,9},{11,10... | collective-permute-start | bytes 786440 | tf_op jit(solution)/shard_map/ppermute | solution.py:177
  34.8 0.2 collective-permute-start.5
  35.0 0.7 collective-permute-start.6
  35.7 6.3 %inside.5 = (bf16[512,2048]{1,0:T(8,128)(2,1)}, f32[2048,512]{1,0:T(8,128)}) custom-call(bf16[3,512,4096]{2,1,0:T(8,128)(2,1)} %q_in.3, bf16[3,3,4096]{2,1,0:T(4,128)(2,1)} %copy-done, f32[3,4,4096]{2,1,0:T(4,128)} %q_taps.3, bf16[512,2048]{1,0:T(8,128)(2,1)} %get-tuple-element.112.refs_3_.k_in, ...), custom_call_target="tpu_custom_call", output_to_operand_aliasing={{0}: (6, {}), {1}: (7, {})} | custom-call | flops 2147483648 | bytes 5242880 | tf_op jit(solution)/shard_map/inside/pallas_call | solution.py:310
  42.1 0.0 copy-done.6
  42.1 0.0 copy-done.1
  42.1 0.0 collective-permute-done.4.rest_2_
  42.1 0.0 copy-start.11
  42.1 0.5 collective-permute-done.5.rest_3_
  42.6 0.0 collective-permute-done.6.rest_1_
  42.6 0.1 add_convert_fusion.1
  42.7 0.1 add_convert_fusion.2
  42.8 1.2 %collective-permute-start.10 = (bf16[8,128,128]{2,1,0:T(8,128)(2,1)S(1)}, bf16[8,128,128]{2,1,0:T(8,128)(2,1)S(1)}, u32[]{:S(2)}, u32[]{:S(2)}) collective-permute-start(bf16[8,128,128]{2,1,0:T(8,128)(2,1)S(1)} %add_convert_fusion.1), channel_id=1, source_target_pairs={{4,0},{5,1},{6,2},{7,3},{0,4},{1,5},{2,6},{3,7},{12,8},{13,9},{14,... | collective-permute-start | bytes 786440 | tf_op jit(solution)/shard_map/ppermute | solution.py:177
  44.0 1.5 %collective-permute-start.7 = (bf16[8,128,128]{2,1,0:T(8,128)(2,1)S(1)}, bf16[8,128,128]{2,1,0:T(8,128)(2,1)S(1)}, u32[]{:S(2)}, u32[]{:S(2)}) collective-permute-start(bf16[8,128,128]{2,1,0:T(8,128)(2,1)S(1)} %collective-permute-done.5.rest_3_), channel_id=1, source_target_pairs={{1,0},{0,1},{3,2},{2,3},{5,4},{4,5},{7,6},{6,7},{9,8},{8,9},{11,10... | collective-permute-start | bytes 786440 | tf_op jit(solution)/shard_map/ppermute | solution.py:177
  45.5 1.3 %collective-permute-start.8 = (bf16[8,128,128]{2,1,0:T(8,128)(2,1)S(1)}, bf16[8,128,128]{2,1,0:T(8,128)(2,1)S(1)}, u32[]{:S(2)}, u32[]{:S(2)}) collective-permute-start(bf16[8,128,128]{2,1,0:T(8,128)(2,1)S(1)} %add_convert_fusion.2), channel_id=1, source_target_pairs={{0,8},{1,9},{2,10},{3,11},{4,12},{5,13},{6,14},{7,15},{16,24},{17,... | collective-permute-start | bytes 786440 | tf_op jit(solution)/shard_map/ppermute | solution.py:177
  46.8 0.1 collective-permute-start.9
  46.9 6.3 %inside.6 = (bf16[512,2048]{1,0:T(8,128)(2,1)}, f32[2048,512]{1,0:T(8,128)}) custom-call(bf16[3,512,4096]{2,1,0:T(8,128)(2,1)} %q_in.3, bf16[3,3,4096]{2,1,0:T(4,128)(2,1)} %copy-done, f32[3,4,4096]{2,1,0:T(4,128)} %q_taps.3, bf16[512,2048]{1,0:T(8,128)(2,1)} %get-tuple-element.145.refs_3_.k_in, bf16[2048,512]{1,0:T(8,128)(2,1)} %get-tuple-element.146.refs_4_.vt_in, ...), custom_call_target="tpu_custom_call" | custom-call | flops 2147483648 | bytes 5242880 | tf_op jit(solution)/shard_map/inside/pallas_call | solution.py:310
  53.2 0.0 copy-done.11
  53.2 0.0 collective-permute-done.10.rest_3_
  53.2 0.0 collective-permute-done.7.rest_4_
  53.2 0.0 copy-start.12
  53.3 8.9 %collective-permute-done.8.rest_5_ = bf16[8,128,128]{2,1,0:T(8,128)(2,1)S(1)} collective-permute-done((bf16[8,128,128]{2,1,0:T(8,128)(2,1)S(1)}, bf16[8,128,128]{2,1,0:T(8,128)(2,1)S(1)}, u32[]{:S(2)}, u32[]{:S(2)}) %collective-permute-start.8) | collective-permute-done | bytes 262176 | tf_op jit(solution)/shard_map/ppermute | solution.py:177
  62.1 0.0 collective-permute-done.9.rest_2_
  62.1 0.1 add_convert_fusion
  62.2 2.3 %collective-permute-start.11 = (bf16[8,128,128]{2,1,0:T(8,128)(2,1)S(1)}, bf16[8,128,128]{2,1,0:T(8,128)(2,1)S(1)}, u32[]{:S(2)}, u32[]{:S(2)}) collective-permute-start(bf16[8,128,128]{2,1,0:T(8,128)(2,1)S(1)} %collective-permute-done.8.rest_5_), channel_id=1, source_target_pairs={{9,8},{8,9},{11,10},{10,11},{13,12},{12,13},{15,14},{14,15},{25,24... | collective-permute-start | bytes 786440 | tf_op jit(solution)/shard_map/ppermute | solution.py:177
  64.6 0.1 collective-permute-start.12
  64.7 1.3 %collective-permute-start.13 = (bf16[8,128,128]{2,1,0:T(8,128)(2,1)S(1)}, bf16[8,128,128]{2,1,0:T(8,128)(2,1)S(1)}, u32[]{:S(2)}, u32[]{:S(2)}) collective-permute-start(bf16[8,128,128]{2,1,0:T(8,128)(2,1)S(1)} %add_convert_fusion), channel_id=1, source_target_pairs={{0,8},{1,9},{2,10},{3,11},{4,12},{5,13},{6,14},{7,15},{16,24},{17,... | collective-permute-start | bytes 786440 | tf_op jit(solution)/shard_map/ppermute | solution.py:177
  66.0 6.3 %inside.7 = (bf16[512,2048]{1,0:T(8,128)(2,1)}, f32[2048,512]{1,0:T(8,128)}) custom-call(bf16[3,512,4096]{2,1,0:T(8,128)(2,1)} %q_in.3, bf16[3,3,4096]{2,1,0:T(4,128)(2,1)} %copy-done, f32[3,4,4096]{2,1,0:T(4,128)} %q_taps.3, bf16[512,2048]{1,0:T(8,128)(2,1)} %get-tuple-element.145.refs_3_.k_in, ...), custom_call_target="tpu_custom_call", output_to_operand_aliasing={{0}: (6, {}), {1}: (7, {})} | custom-call | flops 2147483648 | bytes 5242880 | tf_op jit(solution)/shard_map/inside/pallas_call | solution.py:310
  72.3 0.0 copy-done.4
  72.3 0.0 copy-done.12
  72.3 0.0 copy-done.13
  72.3 0.0 copy-done.7
  72.3 0.0 collective-permute-done.11.rest_6_
  72.4 0.0 collective-permute-done.12.rest_4_
  72.4 2.6 %collective-permute-done.13.rest_5_ = bf16[8,128,128]{2,1,0:T(8,128)(2,1)S(1)} collective-permute-done((bf16[8,128,128]{2,1,0:T(8,128)(2,1)S(1)}, bf16[8,128,128]{2,1,0:T(8,128)(2,1)S(1)}, u32[]{:S(2)}, u32[]{:S(2)}) %collective-permute-start.13) | collective-permute-done | bytes 262176 | tf_op jit(solution)/shard_map/ppermute | solution.py:177
  75.0 3.1 %collective-permute-start.14 = (bf16[8,128,128]{2,1,0:T(8,128)(2,1)S(1)}, bf16[8,128,128]{2,1,0:T(8,128)(2,1)S(1)}, u32[]{:S(2)}, u32[]{:S(2)}) collective-permute-start(bf16[8,128,128]{2,1,0:T(8,128)(2,1)S(1)} %collective-permute-done.13.rest_5_), channel_id=1, source_target_pairs={{9,8},{8,9},{11,10},{10,11},{13,12},{12,13},{15,14},{14,15},{25,24... | collective-permute-start | bytes 786440 | tf_op jit(solution)/shard_map/ppermute | solution.py:177
  78.2 0.5 iota_xor_fusion.order
  78.7 0.0 copy-done.14
  78.7 8.1 %mix.2.rest_7_ = bf16[512,4096]{1,0:T(8,128)(2,1)} custom-call(s32[4]{0:T(128)} %iota_xor_fusion.order, bf16[512,2048]{1,0:T(8,128)(2,1)} %get-tuple-element.179.q_in, f32[2048,512]{1,0:T(8,128)} %get-tuple-element.180.in_in, f32[32,14,512]{2,1,0:T(8,128)} %fusion.2.refs_5_.lam_in, f32[1,4096]{1,0:T(1,128)} %bitcast.3, bf16[16,128,128]{2,1,0:T(8,128)(2,1)} %copy-done.2, ...), custom_call_target="tpu_custom_call" | custom-call | flops 1073741824 | bytes 8388608 | tf_op jit(solution)/shard_map/mix/pallas_call | solution.py:329
  86.8 0.0 collective-permute-done.14.rest_6_
  86.8 0.0 copy-start.10
  86.8 0.7 copy-done.10
  87.5 8.1 %mix.3 = bf16[512,4096]{1,0:T(8,128)(2,1)} custom-call(s32[4]{0:T(128)} %iota_xor_fusion.order, bf16[512,2048]{1,0:T(8,128)(2,1)} %get-tuple-element.167.q_in, f32[2048,512]{1,0:T(8,128)} %get-tuple-element.168.in_in, f32[32,14,512]{2,1,0:T(8,128)} %fusion.2.refs_5_.lam_in, f32[1,4096]{1,0:T(1,128)} %bitcast.4, ...), custom_call_target="tpu_custom_call", output_to_operand_aliasing={{}: (12, {})} | custom-call | flops 1073741824 | bytes 8388608 | tf_op jit(solution)/shard_map/mix/pallas_call | solution.py:329
  (18 shorter events, 0.0 us)
Async XLA Ops:
  1.0 6.6 %collective-permute-start = (bf16[3,3,4096]{2,1,0:T(4,128)(2,1)S(1)}, bf16[3,3,4096]{2,1,0:T(4,128)(2,1)S(1)}, u32[]{:S(2)}, u32[]{:S(2)}) collective-permute-start(bf16[3,3,4096]{2,1,0:T(4,128)(2,1)S(1)} %slice.3), channel_id=1, source_target_pairs={{0,1},{1,2},{2,3},{3,4},{4,5},{5,6},{6,7},{7,8},{8,9},{9,10},{10,1... | collective-permute-start | bytes 221192 | tf_op jit(solution)/shard_map/ppermute | solution.py:236
  7.6 0.6 copy-start
  16.5 9.2 %collective-permute-start.1 = (bf16[16,128,128]{2,1,0:T(8,128)(2,1)}, bf16[16,128,128]{2,1,0:T(8,128)(2,1)S(1)}, u32[]{:S(2)}, u32[]{:S(2)}) collective-permute-start(bf16[16,128,128]{2,1,0:T(8,128)(2,1)} %get-tuple-element.105), channel_id=1, source_target_pairs={{1,0},{0,1},{3,2},{2,3},{5,4},{4,5},{7,6},{6,7},{9,8},{8,9},{11,10... | collective-permute-start | bytes 1572872 | tf_op jit(solution)/shard_map/ppermute | solution.py:177
  17.4 8.2 %copy-start.16 = (bf16[16,128,128]{2,1,0:T(8,128)(2,1)S(1)}, bf16[16,128,128]{2,1,0:T(8,128)(2,1)}, u32[]{:S(2)}) copy-start(bf16[16,128,128]{2,1,0:T(8,128)(2,1)} %get-tuple-element.105) | copy-start | bytes 1572868
  25.6 6.9 %copy-start.2 = (bf16[16,128,128]{2,1,0:T(8,128)(2,1)}, bf16[16,128,128]{2,1,0:T(8,128)(2,1)S(1)}, u32[]{:S(2)}) copy-start(bf16[16,128,128]{2,1,0:T(8,128)(2,1)S(1)} %collective-permute-done.1.rest_0_) | copy-start | bytes 1572868
  25.7 7.6 %collective-permute-start.3 = (bf16[16,128,128]{2,1,0:T(8,128)(2,1)}, bf16[16,128,128]{2,1,0:T(8,128)(2,1)S(1)}, u32[]{:S(2)}, u32[]{:S(2)}) collective-permute-start(bf16[16,128,128]{2,1,0:T(8,128)(2,1)} %get-tuple-element.118), channel_id=1, source_target_pairs={{1,0},{0,1},{3,2},{2,3},{5,4},{4,5},{7,6},{6,7},{9,8},{8,9},{11,10... | collective-permute-start | bytes 1572872 | tf_op jit(solution)/shard_map/ppermute | solution.py:177
  25.8 7.5 %collective-permute-start.2 = (bf16[8,128,128]{2,1,0:T(8,128)(2,1)S(1)}, bf16[8,128,128]{2,1,0:T(8,128)(2,1)S(1)}, u32[]{:S(2)}, u32[]{:S(2)}) collective-permute-start(bf16[8,128,128]{2,1,0:T(8,128)(2,1)S(1)} %add_convert_fusion.5), channel_id=1, source_target_pairs={{2,0},{3,1},{0,2},{1,3},{6,4},{7,5},{4,6},{5,7},{10,8},{11,9},{8,1... | collective-permute-start | bytes 786440 | tf_op jit(solution)/shard_map/ppermute | solution.py:177
  26.2 7.1 %copy-start.15 = (bf16[16,128,128]{2,1,0:T(8,128)(2,1)S(1)}, bf16[16,128,128]{2,1,0:T(8,128)(2,1)}, u32[]{:S(2)}) copy-start(bf16[16,128,128]{2,1,0:T(8,128)(2,1)} %get-tuple-element.118) | copy-start | bytes 1572868
  33.3 8.8 %copy-start.6 = (bf16[8,128,128]{2,1,0:T(8,128)(2,1)}, bf16[8,128,128]{2,1,0:T(8,128)(2,1)S(1)}, u32[]{:S(2)}) copy-start(bf16[8,128,128]{2,1,0:T(8,128)(2,1)S(1)} %collective-permute-done.2.rest_1_) | copy-start | bytes 786436
  33.3 8.8 %copy-start.1 = (bf16[16,128,128]{2,1,0:T(8,128)(2,1)}, bf16[16,128,128]{2,1,0:T(8,128)(2,1)S(1)}, u32[]{:S(2)}) copy-start(bf16[16,128,128]{2,1,0:T(8,128)(2,1)S(1)} %collective-permute-done.3.rest_0_) | copy-start | bytes 1572868
  33.5 8.6 %collective-permute-start.4 = (bf16[8,128,128]{2,1,0:T(8,128)(2,1)S(1)}, bf16[8,128,128]{2,1,0:T(8,128)(2,1)S(1)}, u32[]{:S(2)}, u32[]{:S(2)}) collective-permute-start(bf16[8,128,128]{2,1,0:T(8,128)(2,1)S(1)} %collective-permute-done.2.rest_1_), channel_id=1, source_target_pairs={{1,0},{0,1},{3,2},{2,3},{5,4},{4,5},{7,6},{6,7},{9,8},{8,9},{11,10... | collective-permute-start | bytes 786440 | tf_op jit(solution)/shard_map/ppermute | solution.py:177
  34.8 7.8 %collective-permute-start.5 = (bf16[8,128,128]{2,1,0:T(8,128)(2,1)S(1)}, bf16[8,128,128]{2,1,0:T(8,128)(2,1)S(1)}, u32[]{:S(2)}, u32[]{:S(2)}) collective-permute-start(bf16[8,128,128]{2,1,0:T(8,128)(2,1)S(1)} %get-tuple-element.132), channel_id=1, source_target_pairs={{4,0},{5,1},{6,2},{7,3},{0,4},{1,5},{2,6},{3,7},{12,8},{13,9},{14,... | collective-permute-start | bytes 786440 | tf_op jit(solution)/shard_map/ppermute | solution.py:177
  35.0 7.6 %collective-permute-start.6 = (bf16[8,128,128]{2,1,0:T(8,128)(2,1)S(1)}, bf16[8,128,128]{2,1,0:T(8,128)(2,1)S(1)}, u32[]{:S(2)}, u32[]{:S(2)}) collective-permute-start(bf16[8,128,128]{2,1,0:T(8,128)(2,1)S(1)} %get-tuple-element.134), channel_id=1, source_target_pairs={{2,0},{3,1},{0,2},{1,3},{6,4},{7,5},{4,6},{5,7},{10,8},{11,9},{8,1... | collective-permute-start | bytes 786440 | tf_op jit(solution)/shard_map/ppermute | solution.py:177
  42.1 11.1 %copy-start.11 = (bf16[8,128,128]{2,1,0:T(8,128)(2,1)}, bf16[8,128,128]{2,1,0:T(8,128)(2,1)S(1)}, u32[]{:S(2)}) copy-start(bf16[8,128,128]{2,1,0:T(8,128)(2,1)S(1)} %collective-permute-done.4.rest_2_) | copy-start | bytes 786436
  42.6 10.6 %copy-start.5 = (bf16[8,128,128]{2,1,0:T(8,128)(2,1)}, bf16[8,128,128]{2,1,0:T(8,128)(2,1)S(1)}, u32[]{:S(2)}) copy-start(bf16[8,128,128]{2,1,0:T(8,128)(2,1)S(1)} %collective-permute-done.5.rest_3_) | copy-start | bytes 786436
  42.6 10.6 %copy-start.3 = (bf16[8,128,128]{2,1,0:T(8,128)(2,1)}, bf16[8,128,128]{2,1,0:T(8,128)(2,1)S(1)}, u32[]{:S(2)}) copy-start(bf16[8,128,128]{2,1,0:T(8,128)(2,1)S(1)} %collective-permute-done.6.rest_1_) | copy-start | bytes 786436
  42.8 10.4 %collective-permute-start.10 = (bf16[8,128,128]{2,1,0:T(8,128)(2,1)S(1)}, bf16[8,128,128]{2,1,0:T(8,128)(2,1)S(1)}, u32[]{:S(2)}, u32[]{:S(2)}) collective-permute-start(bf16[8,128,128]{2,1,0:T(8,128)(2,1)S(1)} %add_convert_fusion.1), channel_id=1, source_target_pairs={{4,0},{5,1},{6,2},{7,3},{0,4},{1,5},{2,6},{3,7},{12,8},{13,9},{14,... | collective-permute-start | bytes 786440 | tf_op jit(solution)/shard_map/ppermute | solution.py:177
  44.0 9.2 %collective-permute-start.7 = (bf16[8,128,128]{2,1,0:T(8,128)(2,1)S(1)}, bf16[8,128,128]{2,1,0:T(8,128)(2,1)S(1)}, u32[]{:S(2)}, u32[]{:S(2)}) collective-permute-start(bf16[8,128,128]{2,1,0:T(8,128)(2,1)S(1)} %collective-permute-done.5.rest_3_), channel_id=1, source_target_pairs={{1,0},{0,1},{3,2},{2,3},{5,4},{4,5},{7,6},{6,7},{9,8},{8,9},{11,10... | collective-permute-start | bytes 786440 | tf_op jit(solution)/shard_map/ppermute | solution.py:177
  45.5 16.6 %collective-permute-start.8 = (bf16[8,128,128]{2,1,0:T(8,128)(2,1)S(1)}, bf16[8,128,128]{2,1,0:T(8,128)(2,1)S(1)}, u32[]{:S(2)}, u32[]{:S(2)}) collective-permute-start(bf16[8,128,128]{2,1,0:T(8,128)(2,1)S(1)} %add_convert_fusion.2), channel_id=1, source_target_pairs={{0,8},{1,9},{2,10},{3,11},{4,12},{5,13},{6,14},{7,15},{16,24},{17,... | collective-permute-start | bytes 786440 | tf_op jit(solution)/shard_map/ppermute | solution.py:177
  46.8 15.3 %collective-permute-start.9 = (bf16[8,128,128]{2,1,0:T(8,128)(2,1)S(1)}, bf16[8,128,128]{2,1,0:T(8,128)(2,1)S(1)}, u32[]{:S(2)}, u32[]{:S(2)}) collective-permute-start(bf16[8,128,128]{2,1,0:T(8,128)(2,1)S(1)} %collective-permute-done.6.rest_1_), channel_id=1, source_target_pairs={{1,0},{0,1},{3,2},{2,3},{5,4},{4,5},{7,6},{6,7},{9,8},{8,9},{11,10... | collective-permute-start | bytes 786440 | tf_op jit(solution)/shard_map/ppermute | solution.py:177
  53.2 19.1 %copy-start.4 = (bf16[8,128,128]{2,1,0:T(8,128)(2,1)}, bf16[8,128,128]{2,1,0:T(8,128)(2,1)S(1)}, u32[]{:S(2)}) copy-start(bf16[8,128,128]{2,1,0:T(8,128)(2,1)S(1)} %collective-permute-done.10.rest_3_) | copy-start | bytes 786436
  53.2 19.1 %copy-start.12 = (bf16[8,128,128]{2,1,0:T(8,128)(2,1)}, bf16[8,128,128]{2,1,0:T(8,128)(2,1)S(1)}, u32[]{:S(2)}) copy-start(bf16[8,128,128]{2,1,0:T(8,128)(2,1)S(1)} %collective-permute-done.7.rest_4_) | copy-start | bytes 786436
  62.1 10.2 %copy-start.13 = (bf16[8,128,128]{2,1,0:T(8,128)(2,1)}, bf16[8,128,128]{2,1,0:T(8,128)(2,1)S(1)}, u32[]{:S(2)}) copy-start(bf16[8,128,128]{2,1,0:T(8,128)(2,1)S(1)} %collective-permute-done.8.rest_5_) | copy-start | bytes 786436
  62.1 10.2 %copy-start.7 = (bf16[8,128,128]{2,1,0:T(8,128)(2,1)}, bf16[8,128,128]{2,1,0:T(8,128)(2,1)S(1)}, u32[]{:S(2)}) copy-start(bf16[8,128,128]{2,1,0:T(8,128)(2,1)S(1)} %collective-permute-done.9.rest_2_) | copy-start | bytes 786436
  62.2 10.1 %collective-permute-start.11 = (bf16[8,128,128]{2,1,0:T(8,128)(2,1)S(1)}, bf16[8,128,128]{2,1,0:T(8,128)(2,1)S(1)}, u32[]{:S(2)}, u32[]{:S(2)}) collective-permute-start(bf16[8,128,128]{2,1,0:T(8,128)(2,1)S(1)} %collective-permute-done.8.rest_5_), channel_id=1, source_target_pairs={{9,8},{8,9},{11,10},{10,11},{13,12},{12,13},{15,14},{14,15},{25,24... | collective-permute-start | bytes 786440 | tf_op jit(solution)/shard_map/ppermute | solution.py:177
  64.6 7.8 %collective-permute-start.12 = (bf16[8,128,128]{2,1,0:T(8,128)(2,1)S(1)}, bf16[8,128,128]{2,1,0:T(8,128)(2,1)S(1)}, u32[]{:S(2)}, u32[]{:S(2)}) collective-permute-start(bf16[8,128,128]{2,1,0:T(8,128)(2,1)S(1)} %collective-permute-done.10.rest_3_), channel_id=1, source_target_pairs={{1,0},{0,1},{3,2},{2,3},{5,4},{4,5},{7,6},{6,7},{9,8},{8,9},{11,10... | collective-permute-start | bytes 786440 | tf_op jit(solution)/shard_map/ppermute | solution.py:177
  64.7 10.3 %collective-permute-start.13 = (bf16[8,128,128]{2,1,0:T(8,128)(2,1)S(1)}, bf16[8,128,128]{2,1,0:T(8,128)(2,1)S(1)}, u32[]{:S(2)}, u32[]{:S(2)}) collective-permute-start(bf16[8,128,128]{2,1,0:T(8,128)(2,1)S(1)} %add_convert_fusion), channel_id=1, source_target_pairs={{0,8},{1,9},{2,10},{3,11},{4,12},{5,13},{6,14},{7,15},{16,24},{17,... | collective-permute-start | bytes 786440 | tf_op jit(solution)/shard_map/ppermute | solution.py:177
  72.3 6.4 %copy-start.14 = (bf16[8,128,128]{2,1,0:T(8,128)(2,1)}, bf16[8,128,128]{2,1,0:T(8,128)(2,1)S(1)}, u32[]{:S(2)}) copy-start(bf16[8,128,128]{2,1,0:T(8,128)(2,1)S(1)} %collective-permute-done.11.rest_6_) | copy-start | bytes 786436
  72.4 14.4 %copy-start.8 = (bf16[8,128,128]{2,1,0:T(8,128)(2,1)}, bf16[8,128,128]{2,1,0:T(8,128)(2,1)S(1)}, u32[]{:S(2)}) copy-start(bf16[8,128,128]{2,1,0:T(8,128)(2,1)S(1)} %collective-permute-done.12.rest_4_) | copy-start | bytes 786436
  75.0 11.8 %copy-start.9 = (bf16[8,128,128]{2,1,0:T(8,128)(2,1)}, bf16[8,128,128]{2,1,0:T(8,128)(2,1)S(1)}, u32[]{:S(2)}) copy-start(bf16[8,128,128]{2,1,0:T(8,128)(2,1)S(1)} %collective-permute-done.13.rest_5_) | copy-start | bytes 786436
  75.0 11.8 %collective-permute-start.14 = (bf16[8,128,128]{2,1,0:T(8,128)(2,1)S(1)}, bf16[8,128,128]{2,1,0:T(8,128)(2,1)S(1)}, u32[]{:S(2)}, u32[]{:S(2)}) collective-permute-start(bf16[8,128,128]{2,1,0:T(8,128)(2,1)S(1)} %collective-permute-done.13.rest_5_), channel_id=1, source_target_pairs={{9,8},{8,9},{11,10},{10,11},{13,12},{12,13},{15,14},{14,15},{25,24... | collective-permute-start | bytes 786440 | tf_op jit(solution)/shard_map/ppermute | solution.py:177
  86.8 0.7 copy-start.10
where the time goes:
time: 96.1 us; the launch traced here: 95.6 us
  Pallas kernels  58 us (60%)
  starting transfers between devices  18.4 us (19%)
  waiting for transfers between devices  12.8 us (13%)
  other arithmetic  3.73 us (4%)
  local copies, waits for them, and re-layouts  2.44 us (3%)
    pallas_call x4, Pallas kernels, inside(): return list(call(projected, rim, conv_weight, keys, values_t, lam, *done))  25.3 us
    pallas_call x2, Pallas kernels, states(): pl.pallas_call(functools.partial(state_kernel, dim), grid=(steps,), in_sp...  16.5 us
    pallas_call x2, Pallas kernels, mix(): pl.pallas_call(kernel, grid_spec=pltpu.PrefetchScalarGridSpec(num_scalar_...  16.2 us
    ppermute x14, starting transfers between devices, exchange(): lax.ppermute(value, 'ctx', [(to ^ away, to) for to in self.takers(bit)])  14.7 us
    ppermute x14, waiting for transfers between devices, exchange(): lax.ppermute(value, 'ctx', [(to ^ away, to) for to in self.takers(bit)])  12.8 us
    ppermute x1, starting transfers between devices, on_device(): lax.ppermute(projected[:, rows - taps + 1:, :], 'ctx', [(c, c + 1) for c...  3.71 us
    div x1, other arithmetic, on_device(): (level_codes * scale[:, None, None]).transpose(1, 0, 2).astype(jnp.float32)  2.76 us
  transfers between devices with their start and end apart: 15, of which 4 were waited for; matrix products, arithmetic and copies ran while one was open for 4% of the time, Pallas kernels for 44%

commit v1 on v0

v1 whole, which is shorter than its diff:
```python
import functools

import jax
import jax.numpy as jnp
from jax import lax
from jax.experimental import pallas as pl
from jax.experimental.pallas import tpu as pltpu
from jax.sharding import PartitionSpec as P

PAD = 8
TILE = 128
MESH = pl.DeviceIdType.MESH
F32, BF16 = jnp.float32, jnp.bfloat16
LAG = {0: 2, 1: 6, 2: 10}
LAST = (5, 3, 2)


def spread(count, dim):
    bits = count.bit_length() - 1
    depth = [0] + [1] * (bits - 2) + [min(2, bits - 1)] if bits > 1 else [0]
    swaps = [("swap", bit, 0) for bit in range(bits)]
    shares = [("share", bit, at) for bit in range(bits) for at in reversed(range(depth[bit]))]
    return bits, depth, swaps + shares


def kernel(sizes, *refs):
    heads, dim, rows, taps, level_count, count, chunk, group = sizes
    bits, depth, moves = spread(count, dim)
    chunks = heads // chunk
    width = heads * dim
    tok_bits = rows.bit_length() - 1
    block = min(2 * TILE, rows)
    blocks = rows // block
    block_bits = blocks.bit_length() - 1
    top = TILE.bit_length() - 1
    strip = PAD.bit_length() - 1
    nodes = [(bit, at) for bit in range(block_bits) for at in range(0, blocks >> bit, 2)]

    projected, conv_weight, codes, gain, out = refs[:5]
    xs, taps_in, code_in, lam, gains, rim, held, outer = refs[5:13]
    keys, values_t, queries_t, inner, within, mixed, state = refs[13:20]
    accs = [state] + list(refs[20 : 20 + bits - 1])
    gots = refs[19 + bits : 19 + 2 * bits]
    send_sem, recv_sem, rim_send, rim_recv, small_sem, kv_sem, q_sem, out_sem = refs[19 + 2 * bits :]

    part = lax.axis_index("groups")
    me = lax.axis_index("ctx")

    def region(level):
        start = 0
        for step in range(level):
            start = start + ((me >> step) & 1) * (dim >> (step + 1))
        return pl.ds(pl.multiple_of(start, dim >> level), dim >> level)

    def transfer(move, g):
        kind, bit, at = moves[move]
        which = pl.ds(g * chunk, chunk)
        if kind == "swap":
            source, target = accs[bit].at[which], gots[bit].at[which, region(depth[bit])]
            to = me ^ (1 << bit)
        else:
            source = target = gots[bit].at[which, region(at + 1)]
            to = me ^ (1 << at)
        return pltpu.make_async_remote_copy(
            src_ref=source,
            dst_ref=target,
            send_sem=send_sem.at[move, g],
            recv_sem=recv_sem.at[move, g],
            device_id=(part, to),
            device_id_type=MESH,
        )

    def small(index):
        pair = [(conv_weight, taps_in), (codes, code_in), (gain, gains)][index]
        return pltpu.make_async_copy(*pair, small_sem.at[index])

    def load(kind, g, sem):
        lanes = pl.ds(g * group * dim, group * dim)
        return pltpu.make_async_copy(projected.at[kind, :, lanes], xs.at[kind, :, lanes], sem)

    def load_kv(g):
        lanes = pl.ds(pl.multiple_of(g * group * dim, group * dim), group * dim)
        return pltpu.make_async_copy(
            projected.at[pl.ds(1, 2), :, lanes], xs.at[pl.ds(1, 2), :, lanes], kv_sem.at[g]
        )

    def load_q(g):
        lanes = pl.ds(pl.multiple_of(g * group * dim, group * dim), group * dim)
        return pltpu.make_async_copy(projected.at[0, :, lanes], xs.at[0, :, lanes], q_sem.at[g])

    def rim_copy(index):
        kinds = [pl.ds(1, 2), pl.ds(0, 1)][index]
        return pltpu.make_async_remote_copy(
            src_ref=projected.at[kinds, pl.ds(rows - PAD, PAD)],
            dst_ref=rim.at[kinds],
            send_sem=rim_send.at[index],
            recv_sem=rim_recv.at[index],
            device_id=(part, me + 1),
            device_id_type=MESH,
        )

    for index in range(3):
        small(index).start()
    for g in range(heads // group):
        load_kv(g).start()
    for g in range(heads // group):
        load_q(g).start()

    barrier = pltpu.get_barrier_semaphore()
    for bit in range(bits):
        pl.semaphore_signal(barrier, inc=1, device_id=(part, me ^ (1 << bit)), device_id_type=MESH)
    odd = me & 1
    beside = me + 2 * odd - 1
    has_beside = (beside >= 0) & (beside < count)

    @pl.when(has_beside)
    def _():
        pl.semaphore_signal(barrier, inc=1, device_id=(part, beside), device_id_type=MESH)

    pl.semaphore_wait(barrier, bits + jnp.where(has_beside, 1, 0))

    @pl.when(me < count - 1)
    def _():
        rim_copy(0).start()
        rim_copy(1).start()

    @pl.when(me == 0)
    def _():
        rim[...] = jnp.zeros_like(rim)

    for index in range(3):
        small(index).wait()
    for level in range(level_count):
        scale = 0.125
        if level > tok_bits:
            scale = ((me >> (level - tok_bits - 1)) & 1).astype(F32) * 0.125
        for tile in range(rows // TILE):
            lanes = slice(tile * TILE, (tile + 1) * TILE)
            lam[level, tile] = code_in[level, :, lanes].astype(F32) * scale

    @pl.when(me > 0)
    def _():
        rim_copy(0).wait_recv()
        rim_copy(1).wait_recv()

    def convolve(kind, head, slot):
        lanes = pl.ds(pl.multiple_of(head * dim, dim), dim)
        line = held.at[slot]
        line[0:PAD, :] = rim[kind, :, lanes].astype(F32)
        own = xs[kind, :, lanes].astype(F32)
        line[PAD : PAD + rows, :] = own
        total = taps_in[kind, taps - 1 : taps, lanes] * own
        for tap in range(taps - 1):
            first = PAD - taps + 1 + tap
            total = total + taps_in[kind, tap : tap + 1, lanes] * line[first : first + rows, :]
        return total.astype(BF16)

    def states(g):
        for index in range(chunk):
            head = g * chunk + index
            key = convolve(1, head, 2 * index)
            keys[head] = key
            value_t = convolve(2, head, 2 * index + 1).T
            values_t[head] = value_t
            sums = []
            for at in range(blocks):
                span = slice(at * block, (at + 1) * block)
                sums.append(jnp.dot(value_t[:, span], key[span], preferred_element_type=F32))
            for number, (bit, at) in enumerate(nodes):
                inner[number, head] = sum(sums[at << bit : (at + 1) << bit]).astype(BF16)
            state[head] = sum(sums).astype(BF16)

    strips = TILE // PAD
    lane8 = lax.broadcasted_iota(jnp.int32, (PAD, TILE), 1)
    row8 = lax.broadcasted_iota(jnp.int32, (PAD, TILE), 0)
    lane_strip = lax.broadcasted_iota(jnp.int32, (strips, TILE), 1) >> strip
    row_strip = lax.broadcasted_iota(jnp.int32, (strips, TILE), 0)

    def lam_row(level, head, span):
        tiles = range(span.start // TILE, span.stop // TILE)
        return jnp.concatenate([lam[level, tile, pl.ds(head, 1), :] for tile in tiles], 1)

    def diagonal(head, tile):
        span = slice(tile * TILE, (tile + 1) * TILE)
        differ = lane_strip ^ row_strip
        wide = jnp.broadcast_to(lam_row(top, head, span), differ.shape)
        for level in range(top - 1, strip, -1):
            wide = jnp.where(differ < 2 ** (level - strip), lam_row(level, head, span), wide)
        outer[:, span] = jnp.where(row_strip <= lane_strip, wide, 0.0)
        differ8 = (lane8 & (PAD - 1)) ^ row8
        near = jnp.broadcast_to(lam_row(strip, head, span), differ8.shape)
        for level in range(strip - 1, -1, -1):
            near = jnp.where(differ8 < 2**level, lam_row(level, head, span), near)
        near = jnp.where(row8 <= (lane8 & (PAD - 1)), near, 0.0)
        own = lane8 >> strip
        return jnp.concatenate(
            [jnp.where(own == number, near, outer[number : number + 1, span]) for number in range(strips)], 0
        )

    def inside(head):
        query_t = convolve(0, head, 2 * chunk).T
        queries_t[head] = query_t
        for at in range(blocks):
            span = slice(at * block, (at + 1) * block)
            scores = jnp.dot(keys[head, span, :], query_t[:, span], preferred_element_type=F32)
            tiles = block // TILE
            columns = []
            for tile in range(tiles):
                place = at * tiles + tile
                lanes = slice(tile * TILE, (tile + 1) * TILE)
                pieces = []
                for other in range(tiles):
                    score = scores[other * TILE : (other + 1) * TILE, lanes]
                    if other > tile:
                        pieces.append(jnp.zeros((TILE, TILE), BF16))
                        continue
                    if other == tile:
                        factor = diagonal(head, place)
                    else:
                        level = top + (other ^ tile).bit_length()
                        factor = lam_row(level, head, slice(place * TILE, (place + 1) * TILE))
                    pieces.append((score * factor).astype(BF16))
                columns.append(jnp.concatenate(pieces, 0))
            left = [values_t[head, :, span]]
            right = [jnp.concatenate(columns, 1)]
            for bit in range(block_bits):
                if at >> bit & 1:
                    node = nodes.index((bit, (at >> bit) - 1))
                    level = block.bit_length() + bit
                    scaled = query_t[:, span].astype(F32) * lam_row(level, head, span)
                    left.append(inner[node, head])
                    right.append(scaled.astype(BF16))
            within[head, :, span] = jnp.dot(
                jnp.concatenate(left, 1), jnp.concatenate(right, 0), preferred_element_type=F32
            )

    def mix(g):
        for index in range(chunk):
            head = g * chunk + index
            lanes = pl.ds(pl.multiple_of(head * dim, dim), dim)
            query_t = queries_t[head].astype(F32)
            right = [
                (query_t * lam_row(tok_bits + 1 + bit, head, slice(0, rows))).astype(BF16)
                for bit in range(bits)
            ]
            left = [gots[bit][head] for bit in range(bits)]
            total = within[head] + jnp.dot(
                jnp.concatenate(left, 1), jnp.concatenate(right, 0), preferred_element_type=F32
            )
            inverse = lax.rsqrt(jnp.mean(total * total, 0, keepdims=True) + 1e-06)
            mixed[:, lanes] = ((total * inverse).T * gains[0:1, lanes]).astype(BF16)

    def store(g):
        lanes = pl.ds(pl.multiple_of(g * chunk * dim, chunk * dim), chunk * dim)
        return pltpu.make_async_copy(mixed.at[:, lanes], out.at[:, lanes], out_sem.at[g])

    lag, at = {}, 0
    for bit in range(bits):
        at += 2 if bit == 0 else 4 if bit < bits - 1 else LAST[0]
        lag[bit] = at
    for move in range(bits, len(moves)):
        _, bit, place = moves[move]
        if bit == bits - 1 and place:
            at += LAST[1]
            lag[move] = at
    finish = max(at + LAST[2], heads - chunks)

    def handle(move, g):
        kind, bit, place = moves[move]
        transfer(move, g).wait_recv()
        if kind == "swap":
            if bit < bits - 1:
                which = pl.ds(g * chunk, chunk)
                size = dim >> depth[bit + 1]
                mine = region(depth[bit + 1])
                if depth[bit + 1] == depth[bit]:
                    old = accs[bit][which]
                else:
                    start = 0
                    for step in range(depth[bit], depth[bit + 1]):
                        start = start + ((me >> step) & 1) * (dim >> (step + 1))
                    old = accs[bit][which, pl.ds(pl.multiple_of(start, size), size), :]
                total = old.astype(F32) + gots[bit][which, mine, :].astype(F32)
                accs[bit + 1][which] = total.astype(BF16)
                transfer(bit + 1, g).start()
            if depth[bit]:
                transfer(moves.index(("share", bit, depth[bit] - 1)), g).start()
        else:
            transfer(moves.index(("share", bit, place - 1)), g).start()

    ordered = sorted(lag, key=lambda move: -lag[move])
    final = [move for move in range(len(moves)) if move not in lag]
    gate = group // chunk

    def step(t, carry):
        @pl.when(t < chunks)
        def _():
            @pl.when(lax.rem(t, gate) == 0)
            def _():
                load_kv(t // gate).wait()

            states(t)
            transfer(0, t).start()

        for move in ordered:
            g = t - lag[move]

            @pl.when((g >= 0) & (g < chunks))
            def _(move=move, g=g):
                handle(move, g)

        @pl.when(t < heads)
        def _():
            @pl.when(lax.rem(t, group) == 0)
            def _():
                load_q(t // group).wait()

            inside(t)

        @pl.when((t >= finish) & (t - finish < chunks))
        def _():
            g = t - finish
            for move in final:
                transfer(move, g).wait_recv()
            mix(g)
            store(g).start()

        return carry

    lax.fori_loop(0, finish + chunks, step, 0)

    def drain(g, carry):
        for move in range(len(moves)):
            transfer(move, g).wait_send()
        store(g).wait()
        return carry

    lax.fori_loop(0, chunks, drain, 0)

    @pl.when(me < count - 1)
    def _():
        rim_copy(0).wait_send()
        rim_copy(1).wait_send()


def on_device(projected, conv_weight, level_codes, out_gain):
    kinds, rows, width = projected.shape
    taps = conv_weight.shape[1]
    level_count, heads = level_codes.shape[:2]
    dim = width // heads
    count = lax.axis_size("ctx")
    chunk, group = 2, 4
    chunks = heads // chunk
    bits, depth, moves = spread(count, dim)
    block = min(2 * TILE, rows)
    nodes = max(1, rows // block - 1)
    sizes = (heads, dim, rows, taps, level_count, count, chunk, group)
    vmem, dma = pltpu.VMEM, pltpu.SemaphoreType.DMA
    scratch = [
        vmem((kinds, rows, width), BF16),
        vmem(conv_weight.shape, F32),
        vmem((level_count, heads, rows), jnp.int32),
        vmem((level_count, rows // TILE, heads, TILE), F32),
        vmem((1, width), F32),
        vmem((kinds, PAD, width), BF16),
        vmem((2 * chunk + 1, PAD + rows, dim), F32),
        vmem((TILE // PAD, rows), F32),
        vmem((heads, rows, dim), BF16),
        vmem((heads, dim, rows), BF16),
        vmem((heads, dim, rows), BF16),
        vmem((nodes, heads, dim, dim), BF16),
        vmem((heads, dim, rows), F32),
        vmem((rows, width), BF16),
        vmem((heads, dim, dim), BF16),
    ]
    scratch += [vmem((heads, dim >> depth[bit], dim), BF16) for bit in range(1, bits)]
    scratch += [vmem((heads, dim, dim), BF16) for _ in range(bits)]
    scratch += [
        dma((len(moves), chunks)),
        dma((len(moves), chunks)),
        dma((2,)),
        dma((2,)),
        dma((3,)),
        dma((heads // group,)),
        dma((heads // group,)),
        dma((chunks,)),
    ]
    anywhere = pl.BlockSpec(memory_space=pl.ANY)
    return pl.pallas_call(
        functools.partial(kernel, sizes),
        in_specs=[anywhere] * 4,
        out_specs=anywhere,
        out_shape=jax.ShapeDtypeStruct((rows, width), BF16),
        scratch_shapes=scratch,
        compiler_params=pltpu.CompilerParams(
            collective_id=0, has_side_effects=True, vmem_limit_bytes=63 * 2**20
        ),
        name="attend",
    )(projected, conv_weight, level_codes, out_gain.reshape(1, width))


def solution(mesh):
    placed = (P(None, ("groups", "ctx"), None), P(), P(None, None, ("groups", "ctx")), P())
    return jax.shard_map(
        on_device, mesh=mesh, in_specs=placed, out_specs=P(("groups", "ctx"), None), check_vma=False
    )
```

time: 96.1 us -> 59.3 us (0.62)
  the two profiles are of different devices: /device:TPU:25 before, /device:TPU:0 now
where the time goes in v1:
time: 59.3 us; the launch traced here: 59.2 us
  Pallas kernels  54.5 us (92%)
  local copies, waits for them, and re-layouts  4.7 us (8%)
    pallas_call x1, Pallas kernels, on_device(): pl.pallas_call(functools.partial(kernel, sizes), in_specs=[anywhere] * 4,...  54.5 us
    unnamed x1, local copies, waits for them, and re-layouts  4.7 us

profile of v1, /device:TPU:0, one launch (start us, length us, event | category | flops | bytes accessed | tf_op | source)
XLA Modules:
  0.0 59.2 jit_solution(5609151265414105479)
XLA Ops:
  0.0 54.5 %attend.1 = bf16[512,4096]{1,0:T(8,128)(2,1)} custom-call(bf16[3,512,4096]{2,1,0:T(8,128)(2,1)} %refs_0_.1, f32[3,4,4096]{2,1,0:T(4,128)} %refs_1_.1, s32[14,32,512]{2,1,0:T(8,128)} %refs_2_.1, f32[1,4096]{1,0:T(1,128)} %bitcast.1), custom_call_target="tpu_custom_call" | custom-call | tf_op jit(solution)/shard_map/attend/pallas_call | solution.py:389
  54.5 4.7 %copy.6 = bf16[512,4096]{1,0:T(8,128)(2,1)} copy(bf16[512,4096]{1,0:T(8,128)(2,1)} %attend.1) | data formatting | bytes 8388608

commit v2 on v1

--- a/solution.py
+++ b/solution.py
@@ -11,7 +11,7 @@
 TILE = 128
 MESH = pl.DeviceIdType.MESH
 F32, BF16 = jnp.float32, jnp.bfloat16
-LAG = {0: 2, 1: 6, 2: 10}
+AHEAD = 2
 LAST = (5, 3, 2)
 
 
@@ -36,12 +36,12 @@
     strip = PAD.bit_length() - 1
     nodes = [(bit, at) for bit in range(block_bits) for at in range(0, blocks >> bit, 2)]
 
-    projected, conv_weight, codes, gain, out = refs[:5]
+    projected, conv_weight, codes, gain, mixed = refs[:5]
     xs, taps_in, code_in, lam, gains, rim, held, outer = refs[5:13]
-    keys, values_t, queries_t, inner, within, mixed, state = refs[13:20]
-    accs = [state] + list(refs[20 : 20 + bits - 1])
-    gots = refs[19 + bits : 19 + 2 * bits]
-    send_sem, recv_sem, rim_send, rim_recv, small_sem, kv_sem, q_sem, out_sem = refs[19 + 2 * bits :]
+    keys, values_t, queries_t, inner, within, state = refs[13:19]
+    accs = [state] + list(refs[19 : 19 + bits - 1])
+    gots = refs[18 + bits : 18 + 2 * bits]
+    send_sem, recv_sem, rim_send, rim_recv, small_sem, kv_sem, q_sem = refs[18 + 2 * bits :]
 
     part = lax.axis_index("groups")
     me = lax.axis_index("ctx")
@@ -89,10 +89,11 @@
         return pltpu.make_async_copy(projected.at[0, :, lanes], xs.at[0, :, lanes], q_sem.at[g])
 
     def rim_copy(index):
-        kinds = [pl.ds(1, 2), pl.ds(0, 1)][index]
+        first = group * dim
+        lanes = [pl.ds(0, first), pl.ds(first, width - first)][index]
         return pltpu.make_async_remote_copy(
-            src_ref=projected.at[kinds, pl.ds(rows - PAD, PAD)],
-            dst_ref=rim.at[kinds],
+            src_ref=projected.at[:, pl.ds(rows - PAD, PAD), lanes],
+            dst_ref=rim.at[:, :, lanes],
             send_sem=rim_send.at[index],
             recv_sem=rim_recv.at[index],
             device_id=(part, me + 1),
@@ -141,7 +142,6 @@
     @pl.when(me > 0)
     def _():
         rim_copy(0).wait_recv()
-        rim_copy(1).wait_recv()
 
     def convolve(kind, head, slot):
         lanes = pl.ds(pl.multiple_of(head * dim, dim), dim)
@@ -180,13 +180,13 @@
         tiles = range(span.start // TILE, span.stop // TILE)
         return jnp.concatenate([lam[level, tile, pl.ds(head, 1), :] for tile in tiles], 1)
 
-    def diagonal(head, tile):
+    def diagonal(head, tile, slot):
         span = slice(tile * TILE, (tile + 1) * TILE)
         differ = lane_strip ^ row_strip
         wide = jnp.broadcast_to(lam_row(top, head, span), differ.shape)
         for level in range(top - 1, strip, -1):
             wide = jnp.where(differ < 2 ** (level - strip), lam_row(level, head, span), wide)
-        outer[:, span] = jnp.where(row_strip <= lane_strip, wide, 0.0)
+        outer[slot, :, span] = jnp.where(row_strip <= lane_strip, wide, 0.0)
         differ8 = (lane8 & (PAD - 1)) ^ row8
         near = jnp.broadcast_to(lam_row(strip, head, span), differ8.shape)
         for level in range(strip - 1, -1, -1):
@@ -194,11 +194,11 @@
         near = jnp.where(row8 <= (lane8 & (PAD - 1)), near, 0.0)
         own = lane8 >> strip
         return jnp.concatenate(
-            [jnp.where(own == number, near, outer[number : number + 1, span]) for number in range(strips)], 0
+            [jnp.where(own == number, near, outer[slot, number : number + 1, span]) for number in range(strips)], 0
         )
 
-    def inside(head):
-        query_t = convolve(0, head, 2 * chunk).T
+    def inside(head, slot):
+        query_t = convolve(0, head, 2 * chunk + slot).T
         queries_t[head] = query_t
         for at in range(blocks):
             span = slice(at * block, (at + 1) * block)
@@ -215,7 +215,7 @@
                         pieces.append(jnp.zeros((TILE, TILE), BF16))
                         continue
                     if other == tile:
-                        factor = diagonal(head, place)
+                        factor = diagonal(head, place, slot)
                     else:
                         level = top + (other ^ tile).bit_length()
                         factor = lam_row(level, head, slice(place * TILE, (place + 1) * TILE))
@@ -250,11 +250,7 @@
             inverse = lax.rsqrt(jnp.mean(total * total, 0, keepdims=True) + 1e-06)
             mixed[:, lanes] = ((total * inverse).T * gains[0:1, lanes]).astype(BF16)
 
-    def store(g):
-        lanes = pl.ds(pl.multiple_of(g * chunk * dim, chunk * dim), chunk * dim)
-        return pltpu.make_async_copy(mixed.at[:, lanes], out.at[:, lanes], out_sem.at[g])
-
-    lag, at = {}, 0
+    lag, at = {}, -AHEAD
     for bit in range(bits):
         at += 2 if bit == 0 else 4 if bit < bits - 1 else LAST[0]
         lag[bit] = at
@@ -263,7 +259,7 @@
         if bit == bits - 1 and place:
             at += LAST[1]
             lag[move] = at
-    finish = max(at + LAST[2], heads - chunks)
+    finish = max(at + LAST[2], 1)
 
     def handle(move, g):
         kind, bit, place = moves[move]
@@ -292,16 +288,28 @@
     final = [move for move in range(len(moves)) if move not in lag]
     gate = group // chunk
 
+    def fetch(g, load):
+        @pl.when(lax.rem(g, gate) == 0)
+        def _():
+            load(g // gate).wait()
+
+    def inside_of(g):
+        for index in range(chunk):
+            inside(g * chunk + index, index)
+
+    def early(t, carry):
+        fetch(t, load_kv)
+        states(t)
+        transfer(0, t).start()
+        return carry
+
+    lax.fori_loop(0, AHEAD, early, 0)
+
+    @pl.when(me > 0)
+    def _():
+        rim_copy(1).wait_recv()
+
     def step(t, carry):
-        @pl.when(t < chunks)
-        def _():
-            @pl.when(lax.rem(t, gate) == 0)
-            def _():
-                load_kv(t // gate).wait()
-
-            states(t)
-            transfer(0, t).start()
-
         for move in ordered:
             g = t - lag[move]
 
@@ -309,13 +317,20 @@
             def _(move=move, g=g):
                 handle(move, g)
 
-        @pl.when(t < heads)
+        @pl.when(t < chunks)
         def _():
-            @pl.when(lax.rem(t, group) == 0)
-            def _():
-                load_q(t // group).wait()
-
-            inside(t)
+            fetch(t, load_q)
+
+        @pl.when(t < chunks - AHEAD)
+        def _():
+            fetch(t + AHEAD, load_kv)
+            states(t + AHEAD)
+            inside_of(t)
+            transfer(0, t + AHEAD).start()
+
+        @pl.when((t >= chunks - AHEAD) & (t < chunks))
+        def _():
+            inside_of(t)
 
         @pl.when((t >= finish) & (t - finish < chunks))
         def _():
@@ -323,7 +338,6 @@
             for move in final:
                 transfer(move, g).wait_recv()
             mix(g)
-            store(g).start()
 
         return carry
 
@@ -332,7 +346,6 @@
     def drain(g, carry):
         for move in range(len(moves)):
             transfer(move, g).wait_send()
-        store(g).wait()
         return carry
 
     lax.fori_loop(0, chunks, drain, 0)
@@ -363,14 +376,13 @@
         vmem((level_count, rows // TILE, heads, TILE), F32),
         vmem((1, width), F32),
         vmem((kinds, PAD, width), BF16),
-        vmem((2 * chunk + 1, PAD + rows, dim), F32),
-        vmem((TILE // PAD, rows), F32),
+        vmem((3 * chunk, PAD + rows, dim), F32),
+        vmem((chunk, TILE // PAD, rows), F32),
         vmem((heads, rows, dim), BF16),
         vmem((heads, dim, rows), BF16),
         vmem((heads, dim, rows), BF16),
         vmem((nodes, heads, dim, dim), BF16),
         vmem((heads, dim, rows), F32),
-        vmem((rows, width), BF16),
         vmem((heads, dim, dim), BF16),
     ]
     scratch += [vmem((heads, dim >> depth[bit], dim), BF16) for bit in range(1, bits)]
@@ -383,20 +395,40 @@
         dma((3,)),
         dma((heads // group,)),
         dma((heads // group,)),
-        dma((chunks,)),
     ]
     anywhere = pl.BlockSpec(memory_space=pl.ANY)
-    return pl.pallas_call(
+    mixed = pl.pallas_call(
         functools.partial(kernel, sizes),
         in_specs=[anywhere] * 4,
-        out_specs=anywhere,
-        out_shape=jax.ShapeDtypeStruct((rows, width), BF16),
+        out_specs=pl.BlockSpec(memory_space=pltpu.VMEM),
+        out_shape=vmem((rows, width), BF16),
         scratch_shapes=scratch,
         compiler_params=pltpu.CompilerParams(
-            collective_id=0, has_side_effects=True, vmem_limit_bytes=63 * 2**20
+            collective_id=0, has_side_effects=True, vmem_limit_bytes=56 * 2**20
         ),
         name="attend",
     )(projected, conv_weight, level_codes, out_gain.reshape(1, width))
+    pieces = 8
+
+    def deliver(source, target, sem):
+        def piece(at):
+            span = pl.ds(at * rows // pieces, rows // pieces)
+            return pltpu.make_async_copy(source.at[span], target.at[span], sem.at[at])
+
+        for at in range(pieces):
+            piece(at).start()
+        for at in range(pieces):
+            piece(at).wait()
+
+    return pl.pallas_call(
+        deliver,
+        in_specs=[pl.BlockSpec(memory_space=pltpu.VMEM)],
+        out_specs=anywhere,
+        out_shape=jax.ShapeDtypeStruct((rows, width), BF16),
+        scratch_shapes=[dma((pieces,))],
+        compiler_params=pltpu.CompilerParams(vmem_limit_bytes=2**20),
+        name="deliver",
+    )(mixed)
 
 
 def solution(mesh):

time: 59.3 us -> 51.3 us (0.87)
  local copies, waits for them, and re-layouts: 4.7 us -> 0 us
  Pallas kernels: 54.5 us -> 51.1 us
    pallas_call x1, Pallas kernels: 54.5 us -> 49.1 us  [on_device(): pl.pallas_call(functools.partial(kernel, sizes), in_specs=[anywhere] * 4,...]
    unnamed x1 -> x0, local copies, waits for them, and re-layouts: 4.7 us -> none
    pallas_call x0 -> x1, Pallas kernels: none -> 2.07 us  [on_device(): pl.pallas_call(deliver, in_specs=[pl.BlockSpec(memory_space=pltpu.VMEM)],...]
where the time goes in v2:
time: 51.3 us; the launch traced here: 51.1 us
  Pallas kernels  51.1 us (100%)
    pallas_call x1, Pallas kernels, on_device(): pl.pallas_call(functools.partial(kernel, sizes), in_specs=[anywhere] * 4,...  49.1 us
    pallas_call x1, Pallas kernels, on_device(): pl.pallas_call(deliver, in_specs=[pl.BlockSpec(memory_space=pltpu.VMEM)],...  2.07 us

profile of v2, /device:TPU:0, one launch (start us, length us, event | category | flops | bytes accessed | tf_op | source)
XLA Modules:
  0.0 51.1 jit_solution(12441520560185410577)
XLA Ops:
  0.0 49.1 %attend.1.source = bf16[512,4096]{1,0:T(8,128)(2,1)S(1)} custom-call(bf16[3,512,4096]{2,1,0:T(8,128)(2,1)} %refs_0_.1, f32[3,4,4096]{2,1,0:T(4,128)} %refs_1_.1, s32[14,32,512]{2,1,0:T(8,128)} %refs_2_.1, f32[1,4096]{1,0:T(1,128)} %bitcast.1), custom_call_target="tpu_custom_call" | custom-call | tf_op jit(solution)/shard_map/attend/pallas_call | solution.py:400
  49.1 2.1 %deliver.1 = bf16[512,4096]{1,0:T(8,128)(2,1)} custom-call(bf16[512,4096]{1,0:T(8,128)(2,1)S(1)} %attend.1.source), custom_call_target="tpu_custom_call" | custom-call | tf_op jit(solution)/shard_map/deliver/pallas_call | solution.py:423

commit v3 on v2

--- a/solution.py
+++ b/solution.py
@@ -11,8 +11,9 @@
 TILE = 128
 MESH = pl.DeviceIdType.MESH
 F32, BF16 = jnp.float32, jnp.bfloat16
-AHEAD = 2
-LAST = (5, 3, 2)
+BEHIND = 12
+CHUNK = 2
+INC = (2, 4, 4, 4, 2)
 
 
 def spread(count, dim):
@@ -143,32 +144,45 @@
     def _():
         rim_copy(0).wait_recv()
 
-    def convolve(kind, head, slot):
+    pieces = rows // TILE
+
+    def convolve(kind, head, slot, piece):
         lanes = pl.ds(pl.multiple_of(head * dim, dim), dim)
         line = held.at[slot]
-        line[0:PAD, :] = rim[kind, :, lanes].astype(F32)
-        own = xs[kind, :, lanes].astype(F32)
-        line[PAD : PAD + rows, :] = own
+        start = piece * TILE
+        if piece == 0:
+            line[0:PAD, :] = rim[kind, :, lanes].astype(F32)
+        own = xs[kind, start : start + TILE, lanes].astype(F32)
+        line[PAD + start : PAD + start + TILE, :] = own
         total = taps_in[kind, taps - 1 : taps, lanes] * own
         for tap in range(taps - 1):
-            first = PAD - taps + 1 + tap
-            total = total + taps_in[kind, tap : tap + 1, lanes] * line[first : first + rows, :]
+            first = PAD - taps + 1 + tap + start
+            total = total + taps_in[kind, tap : tap + 1, lanes] * line[first : first + TILE, :]
         return total.astype(BF16)
 
-    def states(g):
-        for index in range(chunk):
-            head = g * chunk + index
-            key = convolve(1, head, 2 * index)
-            keys[head] = key
-            value_t = convolve(2, head, 2 * index + 1).T
-            values_t[head] = value_t
-            sums = []
-            for at in range(blocks):
-                span = slice(at * block, (at + 1) * block)
-                sums.append(jnp.dot(value_t[:, span], key[span], preferred_element_type=F32))
-            for number, (bit, at) in enumerate(nodes):
-                inner[number, head] = sum(sums[at << bit : (at + 1) << bit]).astype(BF16)
-            state[head] = sum(sums).astype(BF16)
+    def states(head, slot):
+        sums, per = [], block // TILE
+        for at in range(blocks):
+            key, value_t = [], []
+            for piece in range(at * per, (at + 1) * per):
+                span = slice(piece * TILE, (piece + 1) * TILE)
+                key.append(convolve(1, head, 2 * slot, piece))
+                keys[head, span, :] = key[-1]
+                yield
+                value_t.append(convolve(2, head, 2 * slot + 1, piece).T)
+                values_t[head, :, span] = value_t[-1]
+                yield
+            sums.append(
+                jnp.dot(
+                    jnp.concatenate(value_t, 1),
+                    jnp.concatenate(key, 0),
+                    preferred_element_type=F32,
+                )
+            )
+            yield
+        for number, (bit, at) in enumerate(nodes):
+            inner[number, head] = sum(sums[at << bit : (at + 1) << bit]).astype(BF16)
+        state[head] = sum(sums).astype(BF16)
 
     strips = TILE // PAD
     lane8 = lax.broadcasted_iota(jnp.int32, (PAD, TILE), 1)
@@ -198,68 +212,100 @@
         )
 
     def inside(head, slot):
-        query_t = convolve(0, head, 2 * chunk + slot).T
-        queries_t[head] = query_t
+        tiles = block // TILE
+        query_t, scores = [], []
+        for at in range(blocks):
+            for piece in range(at * tiles, (at + 1) * tiles):
+                span = slice(piece * TILE, (piece + 1) * TILE)
+                query_t.append(convolve(0, head, 2 * chunk + slot, piece).T)
+                queries_t[head, :, span] = query_t[-1]
+                yield
+            span = slice(at * block, (at + 1) * block)
+            scores.append(
+                jnp.dot(
+                    keys[head, span, :],
+                    jnp.concatenate(query_t[-tiles:], 1),
+                    preferred_element_type=F32,
+                )
+            )
+            yield
         for at in range(blocks):
             span = slice(at * block, (at + 1) * block)
-            scores = jnp.dot(keys[head, span, :], query_t[:, span], preferred_element_type=F32)
-            tiles = block // TILE
             columns = []
             for tile in range(tiles):
                 place = at * tiles + tile
                 lanes = slice(tile * TILE, (tile + 1) * TILE)
-                pieces = []
+                chosen = []
                 for other in range(tiles):
-                    score = scores[other * TILE : (other + 1) * TILE, lanes]
+                    score = scores[at][other * TILE : (other + 1) * TILE, lanes]
                     if other > tile:
-                        pieces.append(jnp.zeros((TILE, TILE), BF16))
+                        chosen.append(jnp.zeros((TILE, TILE), BF16))
                         continue
                     if other == tile:
                         factor = diagonal(head, place, slot)
                     else:
                         level = top + (other ^ tile).bit_length()
                         factor = lam_row(level, head, slice(place * TILE, (place + 1) * TILE))
-                    pieces.append((score * factor).astype(BF16))
-                columns.append(jnp.concatenate(pieces, 0))
+                    chosen.append((score * factor).astype(BF16))
+                    yield
+                columns.append(jnp.concatenate(chosen, 0))
             left = [values_t[head, :, span]]
             right = [jnp.concatenate(columns, 1)]
             for bit in range(block_bits):
                 if at >> bit & 1:
                     node = nodes.index((bit, (at >> bit) - 1))
                     level = block.bit_length() + bit
-                    scaled = query_t[:, span].astype(F32) * lam_row(level, head, span)
+                    query = jnp.concatenate(query_t[at * tiles : (at + 1) * tiles], 1)
+                    scaled = query.astype(F32) * lam_row(level, head, span)
                     left.append(inner[node, head])
                     right.append(scaled.astype(BF16))
             within[head, :, span] = jnp.dot(
                 jnp.concatenate(left, 1), jnp.concatenate(right, 0), preferred_element_type=F32
             )
-
-    def mix(g):
-        for index in range(chunk):
-            head = g * chunk + index
-            lanes = pl.ds(pl.multiple_of(head * dim, dim), dim)
-            query_t = queries_t[head].astype(F32)
-            right = [
-                (query_t * lam_row(tok_bits + 1 + bit, head, slice(0, rows))).astype(BF16)
-                for bit in range(bits)
-            ]
-            left = [gots[bit][head] for bit in range(bits)]
-            total = within[head] + jnp.dot(
-                jnp.concatenate(left, 1), jnp.concatenate(right, 0), preferred_element_type=F32
-            )
-            inverse = lax.rsqrt(jnp.mean(total * total, 0, keepdims=True) + 1e-06)
-            mixed[:, lanes] = ((total * inverse).T * gains[0:1, lanes]).astype(BF16)
-
-    lag, at = {}, -AHEAD
+            yield
+
+    def mix(head, at):
+        lanes = pl.ds(pl.multiple_of(head * dim, dim), dim)
+        span = slice(at * block, (at + 1) * block)
+        query_t = queries_t[head, :, span].astype(F32)
+        right = [
+            (query_t * lam_row(tok_bits + 1 + bit, head, span)).astype(BF16) for bit in range(bits)
+        ]
+        left = [gots[bit][head] for bit in range(bits)]
+        yield
+        total = within[head, :, span] + jnp.dot(
+            jnp.concatenate(left, 1), jnp.concatenate(right, 0), preferred_element_type=F32
+        )
+        yield
+        inverse = lax.rsqrt(jnp.mean(total * total, 0, keepdims=True) + 1e-06)
+        flat = (total * inverse).T
+        yield
+        mixed[span, lanes] = (flat * gains[0:1, lanes]).astype(BF16)
+
+    def together(streams):
+        streams = list(streams)
+        while streams:
+            streams = [stream for stream in streams if next(stream, streams) is not streams]
+
+    def states_of(g):
+        return [states(g * chunk + index, index) for index in range(chunk)]
+
+    def inside_of(g):
+        return [inside(g * chunk + index, index) for index in range(chunk)]
+
+    def mix_of(g):
+        return [mix(g * chunk + index, at) for index in range(chunk) for at in range(blocks)]
+
+    lag, at = {}, 0
     for bit in range(bits):
-        at += 2 if bit == 0 else 4 if bit < bits - 1 else LAST[0]
+        at += INC[min(bit, 1)] if bit < bits - 1 else INC[2]
         lag[bit] = at
     for move in range(bits, len(moves)):
         _, bit, place = moves[move]
         if bit == bits - 1 and place:
-            at += LAST[1]
+            at += INC[3]
             lag[move] = at
-    finish = max(at + LAST[2], 1)
+    finish = at + INC[4]
 
     def handle(move, g):
         kind, bit, place = moves[move]
@@ -293,22 +339,6 @@
         def _():
             load(g // gate).wait()
 
-    def inside_of(g):
-        for index in range(chunk):
-            inside(g * chunk + index, index)
-
-    def early(t, carry):
-        fetch(t, load_kv)
-        states(t)
-        transfer(0, t).start()
-        return carry
-
-    lax.fori_loop(0, AHEAD, early, 0)
-
-    @pl.when(me > 0)
-    def _():
-        rim_copy(1).wait_recv()
-
     def step(t, carry):
         for move in ordered:
             g = t - lag[move]
@@ -317,31 +347,47 @@
             def _(move=move, g=g):
                 handle(move, g)
 
-        @pl.when(t < chunks)
+        @pl.when((t == 1) & (me > 0))
         def _():
-            fetch(t, load_q)
-
-        @pl.when(t < chunks - AHEAD)
+            rim_copy(1).wait_recv()
+
+        works = [(0, load_kv, states_of), (BEHIND, load_q, inside_of), (finish, None, mix_of)]
+        ready = [(t >= late) & (t < late + chunks) for late, _, _ in works]
+        for (late, load, _), here in zip(works, ready):
+            if load:
+
+                @pl.when(here)
+                def _(late=late, load=load):
+                    fetch(t - late, load)
+
+        @pl.when(ready[2])
         def _():
-            fetch(t + AHEAD, load_kv)
-            states(t + AHEAD)
-            inside_of(t)
-            transfer(0, t + AHEAD).start()
-
-        @pl.when((t >= chunks - AHEAD) & (t < chunks))
-        def _():
-            inside_of(t)
-
-        @pl.when((t >= finish) & (t - finish < chunks))
-        def _():
-            g = t - finish
             for move in final:
-                transfer(move, g).wait_recv()
-            mix(g)
+                transfer(move, t - finish).wait_recv()
+
+        for some in range(1, 8):
+            chosen = [some >> place & 1 == 1 for place in range(3)]
+            lates = [late for (late, _, _), own in zip(works, chosen) if own]
+            if max(lates) - min(lates) >= chunks:
+                continue
+            wanted = True
+            for own, here in zip(chosen, ready):
+                wanted = wanted & (here if own else jnp.logical_not(here))
+
+            @pl.when(wanted)
+            def _(chosen=chosen):
+                streams = []
+                for own, (late, _, work) in reversed(list(zip(chosen, works))):
+                    if own:
+                        streams += work(t - late)
+                together(streams)
+
+                if chosen[0]:
+                    transfer(0, t).start()
 
         return carry
 
-    lax.fori_loop(0, finish + chunks, step, 0)
+    lax.fori_loop(0, max(finish, BEHIND) + chunks, step, 0)
 
     def drain(g, carry):
         for move in range(len(moves)):
@@ -362,7 +408,7 @@
     level_count, heads = level_codes.shape[:2]
     dim = width // heads
     count = lax.axis_size("ctx")
-    chunk, group = 2, 4
+    chunk, group = CHUNK, 4
     chunks = heads // chunk
     bits, depth, moves = spread(count, dim)
     block = min(2 * TILE, rows)

time: 51.3 us -> 44.5 us (0.87)
  Pallas kernels: 51.1 us -> 44.4 us
    pallas_call x1, Pallas kernels: 49.1 us -> 42.3 us  [on_device(): pl.pallas_call(functools.partial(kernel, sizes), in_specs=[anywhere] * 4,...]
where the time goes in v3:
time: 44.5 us; the launch traced here: 44.4 us
  Pallas kernels  44.4 us (100%)
    pallas_call x1, Pallas kernels, on_device(): pl.pallas_call(functools.partial(kernel, sizes), in_specs=[anywhere] * 4,...  42.3 us
    pallas_call x1, Pallas kernels, on_device(): pl.pallas_call(deliver, in_specs=[pl.BlockSpec(memory_space=pltpu.VMEM)],...  2.07 us

profile of v3, /device:TPU:0, one launch (start us, length us, event | category | flops | bytes accessed | tf_op | source)
XLA Modules:
  0.0 44.4 jit_solution(13079082211157459604)
XLA Ops:
  0.0 42.3 %attend.1.source = bf16[512,4096]{1,0:T(8,128)(2,1)S(1)} custom-call(bf16[3,512,4096]{2,1,0:T(8,128)(2,1)} %refs_0_.1, f32[3,4,4096]{2,1,0:T(4,128)} %refs_1_.1, s32[14,32,512]{2,1,0:T(8,128)} %refs_2_.1, f32[1,4096]{1,0:T(1,128)} %bitcast.1), custom_call_target="tpu_custom_call" | custom-call | tf_op jit(solution)/shard_map/attend/pallas_call | solution.py:446
  42.3 2.1 %deliver.1 = bf16[512,4096]{1,0:T(8,128)(2,1)} custom-call(bf16[512,4096]{1,0:T(8,128)(2,1)S(1)} %attend.1.source), custom_call_target="tpu_custom_call" | custom-call | tf_op jit(solution)/shard_map/deliver/pallas_call | solution.py:469

commit v4 on v3

--- a/solution.py
+++ b/solution.py
@@ -12,20 +12,58 @@
 MESH = pl.DeviceIdType.MESH
 F32, BF16 = jnp.float32, jnp.bfloat16
 BEHIND = 12
+TAIL = 4
 CHUNK = 2
-INC = (2, 4, 4, 4, 2)
+INC = (2, 4, 4, 0, 4)
 
 
 def spread(count, dim):
     bits = count.bit_length() - 1
     depth = [0] + [1] * (bits - 2) + [min(2, bits - 1)] if bits > 1 else [0]
     swaps = [("swap", bit, 0) for bit in range(bits)]
-    shares = [("share", bit, at) for bit in range(bits) for at in reversed(range(depth[bit]))]
+    shares = [("share", bit, at) for bit in range(bits) for at in range(1, 1 << depth[bit])]
     return bits, depth, swaps + shares
 
 
+def lam_of(lam, level, head, span):
+    tiles = range(span.start // TILE, span.stop // TILE)
+    return jnp.concatenate([lam[level, tile, pl.ds(head, 1), :] for tile in tiles], 1)
+
+
+def mix(shape, refs, out, head, start, at):
+    dim, block, base = shape
+    within, queries_t, lam, gains = refs[:4]
+    gots = refs[4:]
+    span = slice(at * block, (at + 1) * block)
+    query_t = queries_t[head, :, span].astype(F32)
+    right = [
+        (query_t * lam_of(lam, base + bit, head, span)).astype(BF16) for bit in range(len(gots))
+    ]
+    left = [got[head] for got in gots]
+    yield
+    total = within[head, :, span] + jnp.dot(
+        jnp.concatenate(left, 1), jnp.concatenate(right, 0), preferred_element_type=F32
+    )
+    yield
+    inverse = lax.rsqrt(jnp.mean(total * total, 0, keepdims=True) + 1e-06)
+    flat = (total * inverse).T
+    yield
+    out[span, start] = (flat * gains[0:1, lanes_of(head, dim)]).astype(BF16)
+
+
+def lanes_of(head, dim):
+    start = head * dim
+    return pl.ds(start if isinstance(head, int) else pl.multiple_of(start, dim), dim)
+
+
+def together(streams):
+    streams = list(streams)
+    while streams:
+        streams = [stream for stream in streams if next(stream, streams) is not streams]
+
+
 def kernel(sizes, *refs):
-    heads, dim, rows, taps, level_count, count, chunk, group = sizes
+    heads, dim, rows, taps, level_count, count, chunk, group, tail = sizes
     bits, depth, moves = spread(count, dim)
     chunks = heads // chunk
     width = heads * dim
@@ -38,11 +76,12 @@
     nodes = [(bit, at) for bit in range(block_bits) for at in range(0, blocks >> bit, 2)]
 
     projected, conv_weight, codes, gain, mixed = refs[:5]
-    xs, taps_in, code_in, lam, gains, rim, held, outer = refs[5:13]
-    keys, values_t, queries_t, inner, within, state = refs[13:19]
-    accs = [state] + list(refs[19 : 19 + bits - 1])
-    gots = refs[18 + bits : 18 + 2 * bits]
-    send_sem, recv_sem, rim_send, rim_recv, small_sem, kv_sem, q_sem = refs[18 + 2 * bits :]
+    within, queries_t, lam, gains = refs[5:9]
+    gots = refs[9 : 9 + bits]
+    refs = refs[9 + bits :]
+    xs, taps_in, code_in, rim, held, outer, keys, values_t, inner, state = refs[:10]
+    accs = [state] + list(refs[10 : 9 + bits])
+    send_sem, recv_sem, rim_send, rim_recv, small_sem, kv_sem, q_sem = refs[9 + bits :]
 
     part = lax.axis_index("groups")
     me = lax.axis_index("ctx")
@@ -60,8 +99,8 @@
             source, target = accs[bit].at[which], gots[bit].at[which, region(depth[bit])]
             to = me ^ (1 << bit)
         else:
-            source = target = gots[bit].at[which, region(at + 1)]
-            to = me ^ (1 << at)
+            source = target = gots[bit].at[which, region(depth[bit])]
+            to = me ^ at
         return pltpu.make_async_remote_copy(
             src_ref=source,
             dst_ref=target,
@@ -264,29 +303,6 @@
             )
             yield
 
-    def mix(head, at):
-        lanes = pl.ds(pl.multiple_of(head * dim, dim), dim)
-        span = slice(at * block, (at + 1) * block)
-        query_t = queries_t[head, :, span].astype(F32)
-        right = [
-            (query_t * lam_row(tok_bits + 1 + bit, head, span)).astype(BF16) for bit in range(bits)
-        ]
-        left = [gots[bit][head] for bit in range(bits)]
-        yield
-        total = within[head, :, span] + jnp.dot(
-            jnp.concatenate(left, 1), jnp.concatenate(right, 0), preferred_element_type=F32
-        )
-        yield
-        inverse = lax.rsqrt(jnp.mean(total * total, 0, keepdims=True) + 1e-06)
-        flat = (total * inverse).T
-        yield
-        mixed[span, lanes] = (flat * gains[0:1, lanes]).astype(BF16)
-
-    def together(streams):
-        streams = list(streams)
-        while streams:
-            streams = [stream for stream in streams if next(stream, streams) is not streams]
-
     def states_of(g):
         return [states(g * chunk + index, index) for index in range(chunk)]
 
@@ -294,17 +310,18 @@
         return [inside(g * chunk + index, index) for index in range(chunk)]
 
     def mix_of(g):
-        return [mix(g * chunk + index, at) for index in range(chunk) for at in range(blocks)]
+        shape = (dim, block, tok_bits + 1)
+        given = [within, queries_t, lam, gains] + list(gots)
+        return [
+            mix(shape, given, mixed, g * chunk + index, lanes_of(g * chunk + index, dim), at)
+            for index in range(chunk)
+            for at in range(blocks)
+        ]
 
     lag, at = {}, 0
     for bit in range(bits):
         at += INC[min(bit, 1)] if bit < bits - 1 else INC[2]
         lag[bit] = at
-    for move in range(bits, len(moves)):
-        _, bit, place = moves[move]
-        if bit == bits - 1 and place:
-            at += INC[3]
-            lag[move] = at
     finish = at + INC[4]
 
     def handle(move, g):
@@ -325,12 +342,10 @@
                 total = old.astype(F32) + gots[bit][which, mine, :].astype(F32)
                 accs[bit + 1][which] = total.astype(BF16)
                 transfer(bit + 1, g).start()
-            if depth[bit]:
-                transfer(moves.index(("share", bit, depth[bit] - 1)), g).start()
-        else:
-            transfer(moves.index(("share", bit, place - 1)), g).start()
-
-    ordered = sorted(lag, key=lambda move: -lag[move])
+            for share in range(1, 1 << depth[bit]):
+                transfer(moves.index(("share", bit, share)), g).start()
+
+    ordered = sorted(lag, key=lambda move: lag[move])
     final = [move for move in range(len(moves)) if move not in lag]
     gate = group // chunk
 
@@ -351,8 +366,9 @@
         def _():
             rim_copy(1).wait_recv()
 
+        counts = [chunks, chunks, chunks - tail]
         works = [(0, load_kv, states_of), (BEHIND, load_q, inside_of), (finish, None, mix_of)]
-        ready = [(t >= late) & (t < late + chunks) for late, _, _ in works]
+        ready = [(t >= late) & (t < late + many) for (late, _, _), many in zip(works, counts)]
         for (late, load, _), here in zip(works, ready):
             if load:
 
@@ -387,7 +403,12 @@
 
         return carry
 
-    lax.fori_loop(0, max(finish, BEHIND) + chunks, step, 0)
+    last = max(max(lag.values()) + chunks, BEHIND + chunks, finish + chunks - tail)
+    lax.fori_loop(0, last, step, 0)
+
+    for g in range(chunks - tail, chunks):
+        for move in final:
+            transfer(move, g).wait_recv()
 
     def drain(g, carry):
         for move in range(len(moves)):
@@ -408,31 +429,34 @@
     level_count, heads = level_codes.shape[:2]
     dim = width // heads
     count = lax.axis_size("ctx")
-    chunk, group = CHUNK, 4
+    chunk, group, tail = CHUNK, 4, TAIL
     chunks = heads // chunk
     bits, depth, moves = spread(count, dim)
     block = min(2 * TILE, rows)
     nodes = max(1, rows // block - 1)
-    sizes = (heads, dim, rows, taps, level_count, count, chunk, group)
+    sizes = (heads, dim, rows, taps, level_count, count, chunk, group, tail)
     vmem, dma = pltpu.VMEM, pltpu.SemaphoreType.DMA
+    ahead = (chunks - tail) * chunk
+    results = [
+        vmem((rows, ahead * dim), BF16),
+        vmem((heads, dim, rows), F32),
+        vmem((heads, dim, rows), BF16),
+        vmem((level_count, rows // TILE, heads, TILE), F32),
+        vmem((1, width), F32),
+    ] + [vmem((heads, dim, dim), BF16) for _ in range(bits)]
     scratch = [
         vmem((kinds, rows, width), BF16),
         vmem(conv_weight.shape, F32),
         vmem((level_count, heads, rows), jnp.int32),
-        vmem((level_count, rows // TILE, heads, TILE), F32),
-        vmem((1, width), F32),
         vmem((kinds, PAD, width), BF16),
         vmem((3 * chunk, PAD + rows, dim), F32),
         vmem((chunk, TILE // PAD, rows), F32),
         vmem((heads, rows, dim), BF16),
         vmem((heads, dim, rows), BF16),
-        vmem((heads, dim, rows), BF16),
         vmem((nodes, heads, dim, dim), BF16),
-        vmem((heads, dim, rows), F32),
         vmem((heads, dim, dim), BF16),
     ]
     scratch += [vmem((heads, dim >> depth[bit], dim), BF16) for bit in range(1, bits)]
-    scratch += [vmem((heads, dim, dim), BF16) for _ in range(bits)]
     scratch += [
         dma((len(moves), chunks)),
         dma((len(moves), chunks)),
@@ -443,38 +467,58 @@
         dma((heads // group,)),
     ]
     anywhere = pl.BlockSpec(memory_space=pl.ANY)
-    mixed = pl.pallas_call(
+    inside_vmem = pl.BlockSpec(memory_space=pltpu.VMEM)
+    done = pl.pallas_call(
         functools.partial(kernel, sizes),
-        in_specs=[anywhere] * 4,
-        out_specs=pl.BlockSpec(memory_space=pltpu.VMEM),
-        out_shape=vmem((rows, width), BF16),
+        in_specs=[pl.BlockSpec(memory_space=pltpu.HBM)] * 4,
+        out_specs=[inside_vmem] * len(results),
+        out_shape=results,
         scratch_shapes=scratch,
         compiler_params=pltpu.CompilerParams(
-            collective_id=0, has_side_effects=True, vmem_limit_bytes=56 * 2**20
+            collective_id=0, has_side_effects=True, vmem_limit_bytes=34 * 2**20
         ),
         name="attend",
     )(projected, conv_weight, level_codes, out_gain.reshape(1, width))
-    pieces = 8
-
-    def deliver(source, target, sem):
+    tok_bits = rows.bit_length() - 1
+    pieces = ahead * dim // (group * dim)
+
+    def deliver(*refs):
+        mixed, given = refs[0], refs[1 : 5 + bits]
+        target, fresh, sem = refs[5 + bits :]
+
         def piece(at):
-            span = pl.ds(at * rows // pieces, rows // pieces)
-            return pltpu.make_async_copy(source.at[span], target.at[span], sem.at[at])
+            lanes = pl.ds(at * group * dim, group * dim)
+            return pltpu.make_async_copy(mixed.at[:, lanes], target.at[:, lanes], sem.at[at])
+
+        def rest(at):
+            lanes = pl.ds(at * chunk * dim, chunk * dim)
+            lies = pl.ds((ahead + at * chunk) * dim, chunk * dim)
+            return pltpu.make_async_copy(fresh.at[:, lanes], target.at[:, lies], sem.at[pieces + at])
 
         for at in range(pieces):
             piece(at).start()
+        for at in range(tail):
+            heads_here = range(ahead + at * chunk, ahead + (at + 1) * chunk)
+            together(
+                mix((dim, block, tok_bits + 1), given, fresh, head, lanes_of(head - ahead, dim), part)
+                for head in heads_here
+                for part in range(rows // block)
+            )
+            rest(at).start()
         for at in range(pieces):
             piece(at).wait()
+        for at in range(tail):
+            rest(at).wait()
 
     return pl.pallas_call(
         deliver,
-        in_specs=[pl.BlockSpec(memory_space=pltpu.VMEM)],
+        in_specs=[inside_vmem] * len(results),
         out_specs=anywhere,
         out_shape=jax.ShapeDtypeStruct((rows, width), BF16),
-        scratch_shapes=[dma((pieces,))],
-        compiler_params=pltpu.CompilerParams(vmem_limit_bytes=2**20),
+        scratch_shapes=[vmem((rows, max(1, tail * chunk) * dim), BF16), dma((pieces + tail,))],
+        compiler_params=pltpu.CompilerParams(vmem_limit_bytes=4 * 2**20),
         name="deliver",
-    )(mixed)
+    )(*done)
 
 
 def solution(mesh):

time: 44.5 us -> 44.6 us (level)
  local copies, waits for them, and re-layouts: 0 us -> 0.72 us
  Pallas kernels: 44.4 us -> 43.7 us
    unnamed x0 -> x2, local copies, waits for them, and re-layouts: none -> 0.72 us
    pallas_call x2, Pallas kernels: 44.4 us -> 43.7 us  [the longest x1 41.5 us: on_device(): pl.pallas_call(functools.partial(kernel, sizes), in_specs=[pl.BlockSpec(m...]
where the time goes in v4:
time: 44.6 us; the launch traced here: 44.4 us
  Pallas kernels  43.7 us (98%)
  local copies, waits for them, and re-layouts  0.72 us (2%)
    pallas_call x1, Pallas kernels, on_device(): pl.pallas_call(functools.partial(kernel, sizes), in_specs=[pl.BlockSpec(m...  41.5 us
    pallas_call x1, Pallas kernels, on_device(): pl.pallas_call(deliver, in_specs=[inside_vmem] * len(results), out_specs=...  2.15 us

profile of v4, /device:TPU:0, one launch (start us, length us, event | category | flops | bytes accessed | tf_op | source)
XLA Modules:
  0.0 44.4 jit_solution(18165071859098548830)
XLA Ops:
  0.0 0.0 copy-start
  0.0 0.7 %copy-done = f32[4096]{0:T(1024)S(1)} copy-done((f32[4096]{0:T(1024)S(1)}, f32[4096]{0:T(1024)}, u32[]{:S(2)}) %copy-start) | copy-done | bytes 16408
  0.7 41.5 %attend.1 = (bf16[512,3072]{1,0:T(8,128)(2,1)S(1)}, f32[32,128,512]{2,1,0:T(8,128)S(1)}, bf16[32,128,512]{2,1,0:T(8,128)(2,1)S(1)}, f32[14,4,32,128]{3,2,1,0:T(8...) custom-call(bf16[3,512,4096]{2,1,0:T(8,128)(2,1)} %refs_0_.1, ...), custom_call_target="tpu_custom_call" | custom-call | tf_op jit(solution)/shard_map/attend/pallas_call | solution.py:471
  42.3 2.2 %deliver.1 = bf16[512,4096]{1,0:T(8,128)(2,1)} custom-call(bf16[512,3072]{1,0:T(8,128)(2,1)S(1)} %get-tuple-element.14.refs_0_, f32[32,128,512]{2,1,0:T(8,128)S(1)} %get-tuple-element.15.refs_1_, bf16[32,128,512]{2,1,0:T(8,128)(2,1)S(1)} %get-tuple-element.16.refs_2_, f32[14,4,32,128]{3,2,1,0:T(8,128)S(1)} %get-tuple-element.17.refs_3_, ...), custom_call_target="tpu_custom_call" | custom-call | tf_op jit(solution)/shard_map/deliver/pallas_call | solution.py:513
Async XLA Ops:
  0.0 0.7 %copy-start = (f32[4096]{0:T(1024)S(1)}, f32[4096]{0:T(1024)}, u32[]{:S(2)}) copy-start(f32[4096]{0:T(1024)} %param.7) | copy-start | bytes 49156

commit v5 on v4

--- a/solution.py
+++ b/solution.py
@@ -35,9 +35,9 @@
     within, queries_t, lam, gains = refs[:4]
     gots = refs[4:]
     span = slice(at * block, (at + 1) * block)
-    query_t = queries_t[head, :, span].astype(F32)
+    query_t = queries_t[head, :, span]
     right = [
-        (query_t * lam_of(lam, base + bit, head, span)).astype(BF16) for bit in range(len(gots))
+        query_t * lam_of(lam, base + bit, head, span).astype(BF16) for bit in range(len(gots))
     ]
     left = [got[head] for got in gots]
     yield

time: 44.6 us -> 44.4 us (level)
  no operation moved by 1% of the time
where the time goes in v5:
time: 44.4 us; the launch traced here: 44.2 us
  Pallas kernels  43.5 us (98%)
  local copies, waits for them, and re-layouts  0.72 us (2%)
    pallas_call x1, Pallas kernels, on_device(): pl.pallas_call(functools.partial(kernel, sizes), in_specs=[pl.BlockSpec(m...  41.4 us
    pallas_call x1, Pallas kernels, on_device(): pl.pallas_call(deliver, in_specs=[inside_vmem] * len(results), out_specs=...  2.09 us

profile of v5, /device:TPU:0, one launch (start us, length us, event | category | flops | bytes accessed | tf_op | source)
XLA Modules:
  0.0 44.2 jit_solution(11052138178725039911)
XLA Ops:
  0.0 0.0 copy-start
  0.0 0.7 %copy-done = f32[4096]{0:T(1024)S(1)} copy-done((f32[4096]{0:T(1024)S(1)}, f32[4096]{0:T(1024)}, u32[]{:S(2)}) %copy-start) | copy-done | bytes 16408
  0.7 41.4 %attend.1 = (bf16[512,3072]{1,0:T(8,128)(2,1)S(1)}, f32[32,128,512]{2,1,0:T(8,128)S(1)}, bf16[32,128,512]{2,1,0:T(8,128)(2,1)S(1)}, f32[14,4,32,128]{3,2,1,0:T(8...) custom-call(bf16[3,512,4096]{2,1,0:T(8,128)(2,1)} %refs_0_.1, ...), custom_call_target="tpu_custom_call" | custom-call | tf_op jit(solution)/shard_map/attend/pallas_call | solution.py:471
  42.1 2.1 %deliver.1 = bf16[512,4096]{1,0:T(8,128)(2,1)} custom-call(bf16[512,3072]{1,0:T(8,128)(2,1)S(1)} %get-tuple-element.14.refs_0_, f32[32,128,512]{2,1,0:T(8,128)S(1)} %get-tuple-element.15.refs_1_, bf16[32,128,512]{2,1,0:T(8,128)(2,1)S(1)} %get-tuple-element.16.refs_2_, f32[14,4,32,128]{3,2,1,0:T(8,128)S(1)} %get-tuple-element.17.refs_3_, ...), custom_call_target="tpu_custom_call" | custom-call | tf_op jit(solution)/shard_map/deliver/pallas_call | solution.py:513
Async XLA Ops:
  0.0 0.7 %copy-start = (f32[4096]{0:T(1024)S(1)}, f32[4096]{0:T(1024)}, u32[]{:S(2)}) copy-start(f32[4096]{0:T(1024)} %param.7) | copy-start | bytes 49156
